TPU v7x, 32 devices: a whole 2x2x4 slice. The times are simulated.
32 devices in a mesh: dp: 4 (over z), ctx: 8 (over y, x, core).
Axes of the slice: x: 2, y: 2, z: 4, core: 2. Of those that a mesh axis runs over, the one named last changes fastest.
Arguments:
- tokens: bfloat16 [4096, 1152], P(('dp', 'ctx')), may hold values from -6 to 6
- in_gain: bfloat16 [1152], P('dp'), may hold values from 0.099609375 to 1.8984375
- query_weight: bfloat16 [1152, 1024], P('dp'), may hold values from -0.1875 to 0.1875
- key_weight: bfloat16 [1152, 256], P('dp'), may hold values from -0.1875 to 0.1875
- value_weight: bfloat16 [1152, 256], P('dp'), may hold values from -0.1875 to 0.1875
- query_gain: bfloat16 [256], P('dp'), may hold values from 0.099609375 to 1.8984375
- key_gain: bfloat16 [256], P('dp'), may hold values from 0.099609375 to 1.8984375
- out_weight: bfloat16 [1024, 1152], P('dp'), may hold values from -0.75 to 0.75
- attn_post_gain: bfloat16 [1152], P('dp'), may hold values from 0.099609375 to 1.8984375
- ffn_pre_gain: bfloat16 [1152], P('dp'), may hold values from 0.099609375 to 1.8984375
- gate_weight: bfloat16 [1152, 6912], P('dp', 'ctx'), may hold values from -0.1875 to 0.1875
- up_weight: bfloat16 [1152, 6912], P('dp', 'ctx'), may hold values from -0.1875 to 0.1875
- down_weight: bfloat16 [1152, 6912], P('dp', 'ctx'), may hold values from -0.078125 to 0.078125
- ffn_post_gain: bfloat16 [1152], P('dp'), may hold values from 0.099609375 to 1.8984375
- cotangent: bfloat16 [4096, 1152], P(('dp', 'ctx')), may hold values from -6 to 6
Outputs:
- block_out: bfloat16 [4096, 1152], P(('dp', 'ctx'))
- input_grad: float32 [4096, 1152], P(('dp', 'ctx'))
- in_gain_grad: float32 [1152], P('dp')
- query_weight_grad: float32 [1152, 1024], P('dp')
- key_weight_grad: float32 [1152, 256], P('dp')
- value_weight_grad: float32 [1152, 256], P('dp')
- query_gain_grad: float32 [256], P('dp')
- key_gain_grad: float32 [256], P('dp')
- out_weight_grad: float32 [1024, 1152], P('dp')
- attn_post_gain_grad: float32 [1152], P('dp')
- ffn_pre_gain_grad: float32 [1152], P('dp')
- gate_weight_grad: float32 [1152, 6912], P('dp', 'ctx')
- up_weight_grad: float32 [1152, 6912], P('dp', 'ctx')
- down_weight_grad: float32 [1152, 6912], P('dp', 'ctx')
- ffn_post_gain_grad: float32 [1152], P('dp')
All inputs are finite; a program needn't handle non-finite values.
Results may differ from a plain program's by a relative error of at most 0.017.
Values may be sent and summed in bfloat16 or wider, within the bound.
A program may use at most 128 MiB of HBM per device.

v0:
```python
import math

import jax
import jax.numpy as jnp
from jax import lax
from jax.sharding import PartitionSpec as P

HEADS = 4
HEAD = 256


EPS = 1e-06
GELU_C = math.sqrt(2.0 / math.pi)
NEG_FILL = -1e30


def inverse_rms(values):
    return lax.rsqrt(jnp.mean(values * values, axis=-1, keepdims=True) + EPS)


def norm_back(values, scale_inv, gain, grad_out):
    weighted = grad_out * gain
    cubed = scale_inv * scale_inv * scale_inv
    return scale_inv * weighted - values * cubed * jnp.mean(
        weighted * values, axis=-1, keepdims=True
    )


def gelu_pair(values):
    inner = GELU_C * (values + 0.044715 * values * values * values)
    tanh_val = jnp.tanh(inner)
    result = 0.5 * values * (1.0 + tanh_val)
    slope = 0.5 * (1.0 + tanh_val) + 0.5 * values * (1.0 - tanh_val * tanh_val) * GELU_C * (
        1.0 + 3.0 * 0.044715 * values * values
    )
    return (result, slope)


def rotate(values, cosine, sine):
    middle = values.shape[-1] // 2
    first = values[..., :middle]
    second = values[..., middle:]
    return jnp.concatenate(
        [first * cosine - second * sine, second * cosine + first * sine], axis=-1
    )


def unrotate(grads, cosine, sine):
    middle = grads.shape[-1] // 2
    first = grads[..., :middle]
    second = grads[..., middle:]
    return jnp.concatenate(
        [first * cosine + second * sine, second * cosine - first * sine], axis=-1
    )


def rope_tables(positions):
    middle = HEAD // 2
    freqs = jnp.exp(-(2.0 * jnp.arange(middle, dtype=jnp.float32) / HEAD) * math.log(1000000.0))
    angles = positions[:, None] * freqs[None, :]
    return (jnp.cos(angles), jnp.sin(angles))


def matmul(left, right):
    return jnp.dot(left, right, preferred_element_type=jnp.float32)


def matmul_tn(left, right):
    return lax.dot_general(
        left, right, (((0,), (0,)), ((), ())), preferred_element_type=jnp.float32
    )


def matmul_nt(left, right):
    return lax.dot_general(
        left, right, (((1,), (1,)), ((), ())), preferred_element_type=jnp.float32
    )


def gather_attention(
    in_gain,
    query_weight,
    key_weight,
    value_weight,
    query_gain,
    key_gain,
    out_weight,
    attn_post_gain,
    ffn_pre_gain,
    ffn_post_gain,
):
    return (
        lax.all_gather(in_gain, "dp", axis=0, tiled=True),
        lax.all_gather(query_weight, "dp", axis=0, tiled=True),
        lax.all_gather(key_weight, "dp", axis=0, tiled=True),
        lax.all_gather(value_weight, "dp", axis=0, tiled=True),
        lax.all_gather(query_gain, "dp", axis=0, tiled=True),
        lax.all_gather(key_gain, "dp", axis=0, tiled=True),
        lax.all_gather(out_weight, "dp", axis=0, tiled=True),
        lax.all_gather(attn_post_gain, "dp", axis=0, tiled=True),
        lax.all_gather(ffn_pre_gain, "dp", axis=0, tiled=True),
        lax.all_gather(ffn_post_gain, "dp", axis=0, tiled=True),
    )


def gather_ffn(gate_weight, up_weight, down_weight):
    return (
        lax.all_gather(gate_weight, "dp", axis=0, tiled=True),
        lax.all_gather(up_weight, "dp", axis=0, tiled=True),
        lax.all_gather(down_weight, "dp", axis=0, tiled=True),
    )


def on_device(
    tokens,
    in_gain,
    query_weight,
    key_weight,
    value_weight,
    query_gain,
    key_gain,
    out_weight,
    attn_post_gain,
    ffn_pre_gain,
    gate_weight,
    up_weight,
    down_weight,
    ffn_post_gain,
    cotangent,
):
    rows = tokens.shape[0]
    scaling = 1.0 / math.sqrt(HEAD)
    ctx_index = lax.axis_index("ctx")
    query_pos = ctx_index * rows + jnp.arange(rows, dtype=jnp.int32)
    cosine, sine = rope_tables(query_pos.astype(jnp.float32))
    gathered = gather_attention(
        in_gain,
        query_weight,
        key_weight,
        value_weight,
        query_gain,
        key_gain,
        out_weight,
        attn_post_gain,
        ffn_pre_gain,
        ffn_post_gain,
    )
    (
        gain_in,
        query_full,
        key_full,
        value_full,
        gain_query,
        gain_key,
        out_full,
        gain_attn,
        gain_pre,
        gain_post,
    ) = gathered
    gain_in = gain_in.astype(jnp.float32)
    gain_query = gain_query.astype(jnp.float32)
    gain_key = gain_key.astype(jnp.float32)
    gain_attn = gain_attn.astype(jnp.float32)
    gain_pre = gain_pre.astype(jnp.float32)
    gain_post = gain_post.astype(jnp.float32)
    inputs_f = tokens.astype(jnp.float32)
    inv_one = inverse_rms(inputs_f)
    normed_one = (inputs_f * inv_one * gain_in).astype(jnp.bfloat16)
    queries = matmul(normed_one, query_full).reshape(rows, HEADS, HEAD)
    keys = matmul(normed_one, key_full)
    values = matmul(normed_one, value_full).astype(jnp.bfloat16)
    inv_query = inverse_rms(queries)
    inv_key = inverse_rms(keys)
    query_rot = (
        rotate(queries * inv_query * gain_query, cosine[:, None, :], sine[:, None, :]) * scaling
    ).astype(jnp.bfloat16)
    key_rot = rotate(keys * inv_key * gain_key, cosine, sine).astype(jnp.bfloat16)
    run_max = jnp.full((HEADS, rows, 1), NEG_FILL, jnp.float32)
    key_piece = lax.all_gather(key_rot, "ctx", axis=0, tiled=True)
    value_piece = lax.all_gather(values, "ctx", axis=0, tiled=True)
    key_pos = jnp.arange(key_piece.shape[0], dtype=jnp.int32)
    allowed = (query_pos[:, None] >= key_pos[None, :])[None]
    scores = jnp.einsum("qhd,kd->hqk", query_rot, key_piece, preferred_element_type=jnp.float32)
    scores = jnp.where(allowed, scores, NEG_FILL)
    new_max = jnp.maximum(run_max, jnp.max(scores, axis=-1, keepdims=True))
    weights = jnp.where(allowed, jnp.exp(scores - new_max), 0.0)
    run_total = jnp.sum(weights, axis=-1, keepdims=True)
    accum = jnp.einsum(
        "hqk,kd->hqd", weights.astype(jnp.bfloat16), value_piece, preferred_element_type=jnp.float32
    )
    run_max, run_total, accum = (new_max, run_total, accum)
    log_total = run_max + jnp.log(run_total)
    attn_heads = jnp.transpose(accum / run_total, (1, 0, 2)).astype(jnp.bfloat16)
    attn_out = attn_heads.reshape(rows, HEADS * HEAD)
    projected = matmul(attn_out, out_full)
    inv_proj = inverse_rms(projected)
    residual = inputs_f + projected * inv_proj * gain_attn
    inv_two = inverse_rms(residual)
    normed_two = (residual * inv_two * gain_pre).astype(jnp.bfloat16)
    gate_full, up_full, down_full = gather_ffn(gate_weight, up_weight, down_weight)
    piece = lax.all_gather(normed_two, "ctx", axis=0, tiled=True)
    gate_piece = matmul(piece, gate_full)
    up_piece = matmul(piece, up_full)
    gelu_val, gelu_der = gelu_pair(gate_piece)
    hidden = (gelu_val * up_piece).astype(jnp.bfloat16)
    ffn_sum = lax.psum_scatter(matmul_nt(hidden, down_full), "ctx", scatter_dimension=0, tiled=True)
    inv_ffn = inverse_rms(ffn_sum)
    block_out = (residual + ffn_sum * inv_ffn * gain_post).astype(jnp.bfloat16)
    cot = cotangent.astype(jnp.float32)
    grad_post = jnp.sum(cot * ffn_sum * inv_ffn, axis=0)
    ffn_sum_grad = norm_back(ffn_sum, inv_ffn, gain_post, cot).astype(jnp.bfloat16)
    gate_full, up_full, down_full = gather_ffn(gate_weight, up_weight, down_weight)
    rows_all, grad_all = (
        lax.all_gather(normed_two, "ctx", axis=0, tiled=True),
        lax.all_gather(ffn_sum_grad, "ctx", axis=0, tiled=True),
    )
    gate = matmul(rows_all, gate_full)
    upper = matmul(rows_all, up_full)
    gelu_val, gelu_der = gelu_pair(gate)
    hidden_again = (gelu_val * upper).astype(jnp.bfloat16)
    hidden_grad = matmul(grad_all, down_full)
    gate_grad = (hidden_grad * upper * gelu_der).astype(jnp.bfloat16)
    up_grad = (hidden_grad * gelu_val).astype(jnp.bfloat16)
    grad_down = matmul_tn(grad_all, hidden_again)
    grad_gate = matmul_tn(rows_all, gate_grad)
    grad_up = matmul_tn(rows_all, up_grad)
    gate_shard, up_shard, down_shard = (
        lax.psum_scatter(grad_gate, "dp", scatter_dimension=0, tiled=True),
        lax.psum_scatter(grad_up, "dp", scatter_dimension=0, tiled=True),
        lax.psum_scatter(grad_down, "dp", scatter_dimension=0, tiled=True),
    )
    normed_two_grad = lax.psum_scatter(
        matmul_nt(gate_grad, gate_full) + matmul_nt(up_grad, up_full),
        "ctx",
        scatter_dimension=0,
        tiled=True,
    )
    grad_pre = jnp.sum(normed_two_grad * residual * inv_two, axis=0)
    residual_grad = cot + norm_back(residual, inv_two, gain_pre, normed_two_grad)
    grad_attn = jnp.sum(residual_grad * projected * inv_proj, axis=0)
    projected_grad = norm_back(projected, inv_proj, gain_attn, residual_grad).astype(jnp.bfloat16)
    gathered = gather_attention(
        in_gain,
        query_weight,
        key_weight,
        value_weight,
        query_gain,
        key_gain,
        out_weight,
        attn_post_gain,
        ffn_pre_gain,
        ffn_post_gain,
    )
    query_full = gathered[1]
    key_full = gathered[2]
    value_full = gathered[3]
    out_full = gathered[6]
    grad_out = matmul_tn(attn_out, projected_grad)
    attn_out_grad = (
        matmul_nt(projected_grad, out_full).astype(jnp.bfloat16).reshape(rows, HEADS, HEAD)
    )
    delta = jnp.sum(attn_out_grad.astype(jnp.float32) * attn_heads.astype(jnp.float32), axis=-1)
    delta = jnp.transpose(delta, (1, 0))[:, :, None]
    key_all, value_all = (
        lax.all_gather(key_rot, "ctx", axis=0, tiled=True),
        lax.all_gather(values, "ctx", axis=0, tiled=True),
    )
    key_pos = jnp.arange(key_all.shape[0], dtype=jnp.int32)
    allowed = (query_pos[:, None] >= key_pos[None, :])[None]
    scores = jnp.einsum("qhd,kd->hqk", query_rot, key_all, preferred_element_type=jnp.float32)
    probs = jnp.where(allowed, jnp.exp(scores - log_total), 0.0)
    prob_grad = jnp.einsum(
        "qhd,kd->hqk", attn_out_grad, value_all, preferred_element_type=jnp.float32
    )
    score_grad = (probs * (prob_grad - delta)).astype(jnp.bfloat16)
    values_part = jnp.einsum(
        "hqk,qhd->kd", probs.astype(jnp.bfloat16), attn_out_grad, preferred_element_type=jnp.float32
    )
    keys_part = jnp.einsum("hqk,qhd->kd", score_grad, query_rot, preferred_element_type=jnp.float32)
    query_rot_grad = jnp.einsum(
        "hqk,kd->qhd", score_grad, key_all, preferred_element_type=jnp.float32
    )
    key_rot_grad, values_grad = (
        lax.psum_scatter(keys_part, "ctx", scatter_dimension=0, tiled=True),
        lax.psum_scatter(values_part, "ctx", scatter_dimension=0, tiled=True),
    )
    query_normed_grad = unrotate(query_rot_grad * scaling, cosine[:, None, :], sine[:, None, :])
    grad_qgain = jnp.sum(query_normed_grad * queries * inv_query, axis=(0, 1))
    query_grad = (
        norm_back(queries, inv_query, gain_query, query_normed_grad)
        .reshape(rows, HEADS * HEAD)
        .astype(jnp.bfloat16)
    )
    key_normed_grad = unrotate(key_rot_grad, cosine, sine)
    grad_kgain = jnp.sum(key_normed_grad * keys * inv_key, axis=0)
    key_grad = norm_back(keys, inv_key, gain_key, key_normed_grad).astype(jnp.bfloat16)
    value_grad = values_grad.astype(jnp.bfloat16)
    grad_query = matmul_tn(normed_one, query_grad)
    grad_key = matmul_tn(normed_one, key_grad)
    grad_value = matmul_tn(normed_one, value_grad)
    normed_one_grad = (
        matmul_nt(query_grad, query_full)
        + matmul_nt(key_grad, key_full)
        + matmul_nt(value_grad, value_full)
    )
    grad_in = jnp.sum(normed_one_grad * inputs_f * inv_one, axis=0)
    input_grad = residual_grad + norm_back(inputs_f, inv_one, gain_in, normed_one_grad)
    shares = (
        lax.psum_scatter(grad_in, "dp", scatter_dimension=0, tiled=True),
        lax.psum_scatter(grad_query, "dp", scatter_dimension=0, tiled=True),
        lax.psum_scatter(grad_key, "dp", scatter_dimension=0, tiled=True),
        lax.psum_scatter(grad_value, "dp", scatter_dimension=0, tiled=True),
        lax.psum_scatter(grad_qgain, "dp", scatter_dimension=0, tiled=True),
        lax.psum_scatter(grad_kgain, "dp", scatter_dimension=0, tiled=True),
        lax.psum_scatter(grad_out, "dp", scatter_dimension=0, tiled=True),
        lax.psum_scatter(grad_attn, "dp", scatter_dimension=0, tiled=True),
        lax.psum_scatter(grad_pre, "dp", scatter_dimension=0, tiled=True),
        lax.psum_scatter(grad_post, "dp", scatter_dimension=0, tiled=True),
    )
    (
        share_in,
        share_query,
        share_key,
        share_value,
        share_qgain,
        share_kgain,
        share_out,
        share_attn,
        share_pre,
        share_post,
    ) = shares
    summed = lax.psum(
        (
            share_in,
            share_query,
            share_key,
            share_value,
            share_qgain,
            share_kgain,
            share_out,
            share_attn,
            share_pre,
            share_post,
        ),
        "ctx",
    )
    return (
        block_out,
        input_grad,
        summed[0],
        summed[1],
        summed[2],
        summed[3],
        summed[4],
        summed[5],
        summed[6],
        summed[7],
        summed[8],
        gate_shard,
        up_shard,
        down_shard,
        summed[9],
    )


def solution(mesh):
    return jax.shard_map(
        on_device,
        mesh=mesh,
        in_specs=(
            P(("dp", "ctx"), None),
            P("dp"),
            P("dp", None),
            P("dp", None),
            P("dp", None),
            P("dp"),
            P("dp"),
            P("dp", None),
            P("dp"),
            P("dp"),
            P("dp", "ctx"),
            P("dp", "ctx"),
            P("dp", "ctx"),
            P("dp"),
            P(("dp", "ctx"), None),
        ),
        out_specs=(
            P(("dp", "ctx"), None),
            P(("dp", "ctx"), None),
            P("dp"),
            P("dp", None),
            P("dp", None),
            P("dp", None),
            P("dp"),
            P("dp"),
            P("dp", None),
            P("dp"),
            P("dp"),
            P("dp", "ctx"),
            P("dp", "ctx"),
            P("dp", "ctx"),
            P("dp"),
        ),
        check_vma=False,
    )
```

profile of v0, /device:TPU:0, one launch (start us, length us, event | category | flops | bytes accessed | tf_op | source)
XLA Modules:
  0.0 1110.3 jit_solution(13123586550292595275)
XLA Ops:
  17.4 22.4 %all-reduce.15 = (bf16[1152]{0:T(1024)(128)(2,1)S(1)}, bf16[256]{0:T(256)(128)(2,1)S(1)}, bf16[256]{0:T(256)(128)(2,1)S(1)}, bf16[1152]{0:T(1024)(128)(2,1)S(1)}...) all-reduce(bf16[1152]{0:T(1024)(128)(2,1)S(1)} %dynamic-update-slic, ...), channel_id=1, replica_groups=mesh['dp'=4,'ctx'=8] {'dp'}, use_global_device_ids=true, to_apply=%add | all-reduce | flops 5120 | bytes 20480
  42.2 22.8 %all_gather.62 = bf16[1152,256]{1,0:T(8,128)(2,1)S(1)} all-gather(bf16[288,256]{1,0:T(8,128)(2,1)S(1)} %copy-done.34), channel_id=1, replica_groups=mesh['dp'=4,'ctx'=8] {'dp'}, dimensions={0}, use_global_device_ids=true | all-gather | bytes 737280 | tf_op jit(solution)/shard_map/all_gather | solution.py:95
  66.9 9.8 all_gather.64
  76.8 21.2 %all_gather.67 = bf16[1152,256]{1,0:T(8,128)(2,1)S(1)} all-gather(bf16[288,256]{1,0:T(8,128)(2,1)S(1)} %copy-done.35), channel_id=1, replica_groups=mesh['dp'=4,'ctx'=8] {'dp'}, dimensions={0}, use_global_device_ids=true | all-gather | bytes 737280 | tf_op jit(solution)/shard_map/all_gather | solution.py:96
  98.3 10.9 all_gather.68
  109.2 2.2 fusion.85
  116.0 13.7 %all-gather.10.cloned.1.call-done = bf16[1024,1152]{1,0:T(8,128)(2,1)} async-done(((bf16[256,1152]{1,0:T(8,128)(2,1)}), bf16[1024,1152]{1,0:T(8,128)(2,1)}) %all-gather.10.cloned.1.call-update) | async-done | bytes 2359312 | tf_op jit(solution)/shard_map/all_gather | solution.py:99
  129.7 2.3 multiply_reduce_fusion.6
  135.8 39.1 %all-gather.14.cloned.1.call-done = bf16[1152,864]{1,0:T(8,128)(2,1)} async-done(((bf16[288,864]{1,0:T(8,128)(2,1)}), bf16[1152,864]{1,0:T(8,128)(2,1)}) %all-gather.14.cloned.1.call-update) | async-done | bytes 1990672 | tf_op jit(solution)/shard_map/all_gather | solution.py:108
  174.9 30.0 %all-gather.12.cloned.1.call-done = bf16[1024,1152]{1,0:T(8,128)(2,1)} async-done(((bf16[128,1152]{1,0:T(8,128)(2,1)}), bf16[1024,1152]{1,0:T(8,128)(2,1)}) %all-gather.12.cloned.1.call-update) | async-done | bytes 2359312 | tf_op jit(solution)/shard_map/all_gather | solution.py:201
  205.0 6.6 fusion.90
  211.6 39.9 %all-gather.16.cloned.1.call-done = bf16[1152,864]{1,0:T(8,128)(2,1)} async-done(((bf16[288,864]{1,0:T(8,128)(2,1)}), bf16[1152,864]{1,0:T(8,128)(2,1)}) %all-gather.16.cloned.1.call-update) | async-done | bytes 1990672 | tf_op jit(solution)/shard_map/all_gather | solution.py:109
  251.5 9.0 multiply_convert_fusion.1
  260.6 36.4 %all-gather.18.cloned.1.call-done = bf16[1152,864]{1,0:T(8,128)(2,1)} async-done(((bf16[288,864]{1,0:T(8,128)(2,1)}), bf16[1152,864]{1,0:T(8,128)(2,1)}) %all-gather.18.cloned.1.call-update) | async-done | bytes 1990672 | tf_op jit(solution)/shard_map/all_gather | solution.py:110
  296.9 7.2 fusion.91
  304.2 52.7 %reduce-scatter.12.cloned.1.call-done = f32[128,1152]{1,0:T(8,128)} async-done(((f32[1024,1152]{1,0:T(8,128)}), f32[128,1152]{1,0:T(8,128)}) %reduce-scatter.12.cloned.1.call-update) | async-done | bytes 589840 | tf_op jit(solution)/shard_map/reduce_scatter | solution.py:206
  359.4 2.2 fusion.30
  361.9 28.8 %all-gather.20.cloned.1.call-done = bf16[1024,1152]{1,0:T(8,128)(2,1)} async-done(((bf16[128,1152]{1,0:T(8,128)(2,1)}), bf16[1024,1152]{1,0:T(8,128)(2,1)}) %all-gather.20.cloned.1.call-update) | async-done | bytes 2359312 | tf_op jit(solution)/shard_map/all_gather | solution.py:215
  390.7 9.3 multiply_convert_fusion
  400.1 2.9 fusion.92
  403.0 4.6 convolution_add_fusion
  408.7 52.9 %reduce-scatter.14.cloned.1.call-done = f32[128,1152]{1,0:T(8,128)} async-done(((f32[1024,1152]{1,0:T(8,128)}), f32[128,1152]{1,0:T(8,128)}) %reduce-scatter.14.cloned.1.call-update) | async-done | bytes 589840 | tf_op jit(solution)/shard_map/reduce_scatter | solution.py:232
  462.9 1.9 multiply_reduce_fusion.1
  471.4 1.8 fusion.8
  475.7 2.4 convolution_bitcast_fusion
  478.1 33.6 %reduce-scatter.16.cloned.1.call-done = f32[128,256]{1,0:T(8,128)} async-done(((f32[1024,256]{1,0:T(8,128)}), f32[128,256]{1,0:T(8,128)}) %reduce-scatter.16.cloned.1.call-update) | async-done | bytes 131088 | tf_op jit(solution)/shard_map/reduce_scatter | solution.py:284
  512.9 1.6 multiply_reduce_fusion.10
  517.1 34.4 %reduce-scatter.18.cloned.1.call-done = f32[128,256]{1,0:T(8,128)} async-done(((f32[1024,256]{1,0:T(8,128)}), f32[128,256]{1,0:T(8,128)}) %reduce-scatter.18.cloned.1.call-update) | async-done | bytes 131088 | tf_op jit(solution)/shard_map/reduce_scatter | solution.py:285
  551.5 2.3 fusion.66
  558.5 3.0 fusion.82
  562.5 2.9 fusion.94
  565.5 1.6 copy-done.57
  567.1 6.2 fusion.95
  573.6 6.1 fusion.96
  579.7 1.6 copy-done.58
  581.3 6.2 fusion.97
  589.1 25.4 %reduce-scatter.24.cloned.1.call-done = f32[288,256]{1,0:T(8,128)} async-done(((f32[1152,256]{1,0:T(8,128)}), f32[288,256]{1,0:T(8,128)}) %reduce-scatter.24.cloned.1.call-update) | async-done | bytes 294928 | tf_op jit(solution)/shard_map/reduce_scatter | solution.py:312
  614.4 86.1 %reduce-scatter.20.cloned.1.call-done = f32[288,1024]{1,0:T(8,128)} async-done(((f32[1152,1024]{1,0:T(8,128)}), f32[288,1024]{1,0:T(8,128)}) %reduce-scatter.20.cloned.1.call-update) | async-done | bytes 1179664 | tf_op jit(solution)/shard_map/reduce_scatter | solution.py:310
  700.5 88.0 %reduce-scatter.26.cloned.1.call-done = f32[256,1152]{1,0:T(8,128)} async-done(((f32[1024,1152]{1,0:T(8,128)}), f32[256,1152]{1,0:T(8,128)}) %reduce-scatter.26.cloned.1.call-update) | async-done | bytes 1179664 | tf_op jit(solution)/shard_map/reduce_scatter | solution.py:315
  788.5 1.7 fusion.93
  791.8 1.6 fusion.42
  793.4 20.7 %all-reduce.14 = (f32[1152]{0:T(1024)S(1)}, f32[256]{0:T(256)S(1)}, f32[256]{0:T(256)S(1)}, f32[1152]{0:T(1024)S(1)}, f32[1152]{0:T(1024)S(1)}, /*index=5*/f32[1152]{0:T(1024)S(1)}) all-reduce(f32[1152]{0:T(1024)S(1)} %get-tuple-element.21, f32[256]{0:T(256)S(1)} %reduce_sum.204, ...), channel_id=6, replica_groups=mesh['dp'=4,'ctx'=8] {'dp'}, use_global_device_ids=true, to_apply=%region_20.21.clone | all-reduce | flops 5120 | bytes 40960
  814.6 12.9 %all-reduce.12 = (f32[288]{0:T(512)}, f32[64]{0:T(128)}, f32[64]{0:T(128)}, f32[288]{0:T(512)}, f32[288]{0:T(512)}, /*index=5*/f32[288]{0:T(512)}) all-reduce(f32[288]{0:T(512)S(1)} %dynamic-slice.7, f32[64]{0:T(128)S(1)} %dynamic-slice.9, f32[64]{0:T(128)S(1)} %dynamic-slice.11, ...), channel_id=1, replica_groups=mesh['dp'=4,'ctx'=8] {'ctx'}, use_global_device_ids=true, to_apply=%region_21.22 | all-reduce | flops 1280 | bytes 10240 | tf_op jit(solution)/shard_map/psum | solution.py:332
  828.6 40.3 %reduce-scatter.28.cloned.1.call-done = f32[288,864]{1,0:T(8,128)} async-done(((f32[1152,864]{1,0:T(8,128)}), f32[288,864]{1,0:T(8,128)}) %reduce-scatter.28.cloned.1.call-update) | async-done | bytes 995344 | tf_op jit(solution)/shard_map/reduce_scatter | solution.py:228
  868.9 78.8 %reduce-scatter.30.cloned.1.call-done = f32[288,864]{1,0:T(8,128)} async-done(((f32[1152,864]{1,0:T(8,128)}), f32[288,864]{1,0:T(8,128)}) %reduce-scatter.30.cloned.1.call-update) | async-done | bytes 995344 | tf_op jit(solution)/shard_map/reduce_scatter | solution.py:229
  947.7 79.0 %reduce-scatter.32.cloned.1.call-done = f32[288,864]{1,0:T(8,128)} async-done(((f32[1152,864]{1,0:T(8,128)}), f32[288,864]{1,0:T(8,128)}) %reduce-scatter.32.cloned.1.call-update) | async-done | bytes 995344 | tf_op jit(solution)/shard_map/reduce_scatter | solution.py:230
  1026.7 71.9 %all-reduce.18.cloned.1.call-done = (f32[288,1024]{1,0:T(8,128)}, f32[288,256]{1,0:T(8,128)}, f32[288,256]{1,0:T(8,128)}, f32[256,1152]{1,0:T(8,128)}) async-done(((f32[288,1024]{1,0:T(8,128)}, f32[288,256]{1,0:T(8,128)}, f32[288,256]{1,0:T(8,128)}, f32[256,1152]{1,0:T(8,128)}), (f32[288,1024]{1,0:T(8,128)}, f32[288,256]{1,0:T(8,128)}, f32[288,256]{1,0:T(8,128)}, ...) | async-done | bytes 2949136 | tf_op jit(solution)/shard_map/psum | solution.py:332
  1098.6 2.5 copy.145
  (259 shorter events, 51.0 us)
Async XLA Ops:
  7.2 57.8 %copy-start = (bf16[128,1152]{1,0:T(8,128)(2,1)S(1)}, bf16[128,1152]{1,0:T(8,128)(2,1)}, u32[]{:S(2)}) copy-start(bf16[128,1152]{1,0:T(8,128)(2,1)} %param.15) | copy-start | bytes 884740
  7.2 35.0 %copy-start.34 = (bf16[288,256]{1,0:T(8,128)(2,1)S(1)}, bf16[288,256]{1,0:T(8,128)(2,1)}, u32[]{:S(2)}) copy-start(bf16[288,256]{1,0:T(8,128)(2,1)} %param.18) | copy-start | bytes 442372
  7.2 102.0 %all-gather.8.cloned.1.call-start = ((), (), s32[]{:S(2)}) async-start(), calls=%async_computation.11 | async-start | bytes 2949120 | tf_op jit(solution)/shard_map/all_gather | solution.py:94
  7.9 68.8 %copy-start.35 = (bf16[288,256]{1,0:T(8,128)(2,1)S(1)}, bf16[288,256]{1,0:T(8,128)(2,1)}, u32[]{:S(2)}) copy-start(bf16[288,256]{1,0:T(8,128)(2,1)} %param.19) | copy-start | bytes 442372
  7.9 121.7 %all-gather.10.cloned.1.call-start = ((), (), s32[]{:S(2)}) async-start(), calls=%async_computation.12 | async-start | bytes 2949120 | tf_op jit(solution)/shard_map/all_gather | solution.py:99
  8.7 166.2 %all-gather.14.cloned.1.call-start = ((), (), s32[]{:S(2)}) async-start(), calls=%async_computation.14 | async-start | bytes 2580480 | tf_op jit(solution)/shard_map/all_gather | solution.py:108
  9.4 195.5 %all-gather.12.cloned.1.call-start = ((), (), s32[]{:S(2)}) async-start(), calls=%async_computation.13 | async-start | bytes 2654208 | tf_op jit(solution)/shard_map/all_gather | solution.py:201
  9.5 88.8 %copy-start.51 = (f32[128]{0:T(128)}, f32[128]{0:T(128)S(1)}, u32[]{:S(2)}) copy-start(f32[128]{0:T(128)S(1)} %multiply_exponential_fusion) | copy-start | bytes 1540
  9.5 88.7 %copy-start.53 = (f32[128]{0:T(128)}, f32[128]{0:T(128)S(1)}, u32[]{:S(2)}) copy-start(f32[128]{0:T(128)S(1)} %fusion.78) | copy-start | bytes 1540
  42.1 67.0 %copy-start.38 = (f32[128]{0:T(128)}, f32[128]{0:T(128)S(1)}, u32[]{:S(2)}) copy-start(f32[128]{0:T(128)S(1)} %get-tuple-element.75) | copy-start | bytes 1540
  42.2 70.4 %copy-start.42 = (f32[256]{0:T(256)}, f32[256]{0:T(256)S(1)}, u32[]{:S(2)}) copy-start(f32[256]{0:T(256)S(1)} %convert_element_type.98) | copy-start | bytes 3076
  65.0 44.2 %copy-start.11 = (bf16[1152,256]{1,0:T(8,128)(2,1)}, bf16[1152,256]{1,0:T(8,128)(2,1)S(1)}, u32[]{:S(2)}) copy-start(bf16[1152,256]{1,0:T(8,128)(2,1)S(1)} %all_gather.62) | copy-start | bytes 1769476
  66.9 45.9 %copy-start.26 = (f32[128,128]{1,0:T(8,128)}, f32[128,128]{1,0:T(8,128)S(1)}, u32[]{:S(2)}) copy-start(f32[128,128]{1,0:T(8,128)S(1)} %get-tuple-element.68) | copy-start | bytes 196612
  66.9 45.9 %copy-start.28 = (f32[128,128]{1,0:T(8,128)}, f32[128,128]{1,0:T(8,128)S(1)}, u32[]{:S(2)}) copy-start(f32[128,128]{1,0:T(8,128)S(1)} %get-tuple-element.69) | copy-start | bytes 196612
  76.8 36.1 %copy-start.7 = (bf16[1024,256]{1,0:T(8,128)(2,1)}, bf16[1024,256]{1,0:T(8,128)(2,1)S(1)}, u32[]{:S(2)}) copy-start(bf16[1024,256]{1,0:T(8,128)(2,1)S(1)} %all_gather.64) | copy-start | bytes 1572868
  97.9 11.2 %copy-start.13 = (bf16[1152,256]{1,0:T(8,128)(2,1)}, bf16[1152,256]{1,0:T(8,128)(2,1)S(1)}, u32[]{:S(2)}) copy-start(bf16[1152,256]{1,0:T(8,128)(2,1)S(1)} %all_gather.67) | copy-start | bytes 1769476
  115.8 16.8 %copy-start.25 = (bf16[128,4,256]{2,0,1:T(8,128)(2,1)}, bf16[128,4,256]{2,0,1:T(8,128)(2,1)S(1)}, u32[]{:S(2)}) copy-start(bf16[128,4,256]{2,0,1:T(8,128)(2,1)S(1)} %fusion.17) | copy-start | bytes 786436
  116.0 16.6 %copy-start.14 = (bf16[128,4,256]{0,2,1:T(8,128)(2,1)}, bf16[128,4,256]{0,2,1:T(8,128)(2,1)S(1)}, u32[]{:S(2)}) copy-start(bf16[128,4,256]{0,2,1:T(8,128)(2,1)S(1)} %copy.104) | copy-start | bytes 786436
  132.5 79.0 %copy-start.46 = (f32[128]{0:T(128)}, f32[128]{0:T(128)S(1)}, u32[]{:S(2)}) copy-start(f32[128]{0:T(128)S(1)} %get-tuple-element.79) | copy-start | bytes 1540
  133.6 78.0 %copy-start.49 = (f32[128]{0:T(128)}, f32[128]{0:T(128)S(1)}, u32[]{:S(2)}) copy-start(f32[128]{0:T(128)S(1)} %get-tuple-element.81) | copy-start | bytes 1540
  134.5 117.1 %all-gather.16.cloned.1.call-start = ((), (), s32[]{:S(2)}) async-start(), calls=%async_computation.15 | async-start | bytes 2580480 | tf_op jit(solution)/shard_map/all_gather | solution.py:109
  135.0 161.9 %all-gather.18.cloned.1.call-start = ((), (), s32[]{:S(2)}) async-start(), calls=%async_computation.16 | async-start | bytes 2580480 | tf_op jit(solution)/shard_map/all_gather | solution.py:110
  135.6 221.2 %reduce-scatter.12.cloned.1.call-start = ((), (), s32[]{:S(2)}) async-start(), calls=%async_computation.17 | async-start | bytes 5308416 | tf_op jit(solution)/shard_map/reduce_scatter | solution.py:206
  304.1 86.6 %all-gather.20.cloned.1.call-start = ((), (), s32[]{:S(2)}) async-start(), calls=%async_computation.18 | async-start | bytes 2654208 | tf_op jit(solution)/shard_map/all_gather | solution.py:215
  361.7 99.9 %reduce-scatter.14.cloned.1.call-start = ((), (), s32[]{:S(2)}) async-start(), calls=%async_computation.19 | async-start | bytes 5308416 | tf_op jit(solution)/shard_map/reduce_scatter | solution.py:232
  407.7 104.0 %reduce-scatter.16.cloned.1.call-start = ((), (), s32[]{:S(2)}) async-start(), calls=%async_computation.20 | async-start | bytes 1179648 | tf_op jit(solution)/shard_map/reduce_scatter | solution.py:284
  475.6 36.1 %copy-start.52 = (f32[128]{0:T(128)S(1)}, f32[128]{0:T(128)}, u32[]{:S(2)}) copy-start(f32[128]{0:T(128)} %copy-done.51) | copy-start | bytes 1540
  475.6 36.1 %copy-start.54 = (f32[128]{0:T(128)S(1)}, f32[128]{0:T(128)}, u32[]{:S(2)}) copy-start(f32[128]{0:T(128)} %copy-done.53) | copy-start | bytes 1540
  475.6 37.3 %copy-start.41 = (f32[256]{0:T(256)S(1)}, f32[256]{0:T(256)}, u32[]{:S(2)}) copy-start(f32[256]{0:T(256)} %copy-done.40) | copy-start | bytes 3076
  475.6 37.3 %copy-start.48 = (f32[128]{0:T(128)S(1)}, f32[128]{0:T(128)}, u32[]{:S(2)}) copy-start(f32[128]{0:T(128)} %copy-done.47) | copy-start | bytes 1540
  475.6 38.9 %copy-start.55 = (f32[128]{0:T(128)S(1)}, f32[128]{0:T(128)}, u32[]{:S(2)}) copy-start(f32[128]{0:T(128)} %get-tuple-element.76) | copy-start | bytes 1540
  475.6 39.9 %copy-start.39 = (f32[128]{0:T(128)S(1)}, f32[128]{0:T(128)}, u32[]{:S(2)}) copy-start(f32[128]{0:T(128)} %copy-done.38) | copy-start | bytes 1540
  475.6 75.8 %reduce-scatter.18.cloned.1.call-start = ((), (), s32[]{:S(2)}) async-start(), calls=%async_computation.21 | async-start | bytes 1179648 | tf_op jit(solution)/shard_map/reduce_scatter | solution.py:285
  478.1 111.0 %reduce-scatter.22.cloned.1.call-start = ((), (), s32[]{:S(2)}) async-start(), calls=%async_computation.23 | async-start | bytes 1474560 | tf_op jit(solution)/shard_map/reduce_scatter | solution.py:311
  515.6 35.9 %copy-start.30 = (bf16[128,256]{1,0:T(8,128)(2,1)}, bf16[128,256]{1,0:T(8,128)(2,1)S(1)}, u32[]{:S(2)}) copy-start(bf16[128,256]{1,0:T(8,128)(2,1)S(1)} %subtract_convert_fusion.2) | copy-start | bytes 196612
  517.0 36.9 %copy-start.43 = (f32[256]{0:T(256)S(1)}, f32[256]{0:T(256)}, u32[]{:S(2)}) copy-start(f32[256]{0:T(256)} %copy-done.42) | copy-start | bytes 3076
  517.0 36.9 %copy-start.37 = (f32[128,4]{0,1:T(4,128)S(1)}, f32[128,4]{0,1:T(4,128)}, u32[]{:S(2)}) copy-start(f32[128,4]{0,1:T(4,128)} %copy-done.36) | copy-start | bytes 6148
  517.0 38.1 %copy-start.45 = (f32[128,4]{0,1:T(4,128)S(1)}, f32[128,4]{0,1:T(4,128)}, u32[]{:S(2)}) copy-start(f32[128,4]{0,1:T(4,128)} %get-tuple-element.66) | copy-start | bytes 6148
  517.1 97.4 %reduce-scatter.24.cloned.1.call-start = ((), (), s32[]{:S(2)}) async-start(), calls=%async_computation.24 | async-start | bytes 1474560 | tf_op jit(solution)/shard_map/reduce_scatter | solution.py:312
  553.9 146.6 %reduce-scatter.20.cloned.1.call-start = ((), (), s32[]{:S(2)}) async-start(), calls=%async_computation.22 | async-start | bytes 5898240 | tf_op jit(solution)/shard_map/reduce_scatter | solution.py:310
  561.6 226.9 %reduce-scatter.26.cloned.1.call-start = ((), (), s32[]{:S(2)}) async-start(), calls=%async_computation.25 | async-start | bytes 5898240 | tf_op jit(solution)/shard_map/reduce_scatter | solution.py:315
  565.4 303.5 %reduce-scatter.28.cloned.1.call-start = ((), (), s32[]{:S(2)}) async-start(), calls=%async_computation.26 | async-start | bytes 5160960 | tf_op jit(solution)/shard_map/reduce_scatter | solution.py:228
  573.3 374.4 %reduce-scatter.30.cloned.1.call-start = ((), (), s32[]{:S(2)}) async-start(), calls=%async_computation.27 | async-start | bytes 5160960 | tf_op jit(solution)/shard_map/reduce_scatter | solution.py:229
  579.7 447.1 %reduce-scatter.32.cloned.1.call-start = ((), (), s32[]{:S(2)}) async-start(), calls=%async_computation.28 | async-start | bytes 5160960 | tf_op jit(solution)/shard_map/reduce_scatter | solution.py:230
  587.5 201.0 %copy-start.3 = (bf16[1152,1024]{1,0:T(8,128)(2,1)S(1)}, bf16[1152,1024]{1,0:T(8,128)(2,1)}, u32[]{:S(2)}) copy-start(bf16[1152,1024]{1,0:T(8,128)(2,1)} %all-gather.8.cloned.1.call-done) | copy-start | bytes 7077892
  587.5 511.0 %all-reduce.18.cloned.1.call-start = ((), (), s32[]{:S(2)}) async-start(), calls=%async_computation.29 | async-start | bytes 5898240 | tf_op jit(solution)/shard_map/psum | solution.py:332
  790.2 37.3 %copy-start.6 = (f32[128,1152]{1,0:T(8,128)S(1)}, f32[128,1152]{1,0:T(8,128)}, u32[]{:S(2)}) copy-start(f32[128,1152]{1,0:T(8,128)} %copy-done.5) | copy-start | bytes 1769476
  790.2 37.3 %copy-start.56 = (f32[128]{0:T(128)S(1)}, f32[128]{0:T(128)}, u32[]{:S(2)}) copy-start(f32[128]{0:T(128)} %get-tuple-element.74) | copy-start | bytes 1540
  (34 other events, 82.8 us)
Sparse Core Ops, SparseCore 0:
  9.6 63.3 all-gather.7
  74.5 55.1 all-gather.9
  131.3 43.6 all-gather.13
  177.2 27.6 all-gather.11
  206.4 45.1 all-gather.15
  253.0 43.9 all-gather.17
  304.2 52.5 reduce-scatter.11
  361.8 28.8 all-gather.19
  407.8 53.7 reduce-scatter.13
  475.7 35.9 reduce-scatter.15
  515.5 35.9 reduce-scatter.17
  554.2 29.3 reduce-scatter.21
  586.5 27.9 reduce-scatter.23
  616.6 83.8 reduce-scatter.19
  702.7 85.7 reduce-scatter.25
  791.3 77.6 reduce-scatter.27
  871.6 76.0 reduce-scatter.29
  950.5 76.2 reduce-scatter.31
  1030.4 68.1 all-reduce.17
where the time goes:
time: 1120 us; the launch traced here: 1110 us
  waiting for transfers between devices  834 us (74%)
  blocking collectives  121 us (11%)
  matrix products  87.9 us (8%)
  local copies, waits for them, and re-layouts  24.7 us (2%)
  other arithmetic  23.1 us (2%)
  between operations  17.8 us (2%)
    reduce_scatter x1, waiting for transfers between devices, on_device(): lax.psum_scatter(grad_out, 'dp', scatter_dimension=0, tiled=True)  88 us
    reduce_scatter x1, waiting for transfers between devices, on_device(): lax.psum_scatter(grad_query, 'dp', scatter_dimension=0, tiled=True)  86.1 us
    reduce_scatter x1, waiting for transfers between devices, on_device(): lax.psum_scatter(grad_down, 'dp', scatter_dimension=0, tiled=True)  79 us
    reduce_scatter x1, waiting for transfers between devices, on_device(): lax.psum_scatter(grad_up, 'dp', scatter_dimension=0, tiled=True)  78.8 us
    psum x1, waiting for transfers between devices, on_device(): lax.psum((share_in, share_query, share_key, share_value, share_qgain, sha...  71.9 us
    reduce_scatter x1, waiting for transfers between devices, on_device(): lax.psum_scatter(matmul_nt(gate_grad, gate_full) + matmul_nt(up_grad, up_...  52.9 us
    reduce_scatter x1, waiting for transfers between devices, on_device(): lax.psum_scatter(matmul_nt(hidden, down_full), 'ctx', scatter_dimension=0...  52.7 us
    unnamed x2, blocking collectives  43.1 us
  transfers between devices with their start and end apart: 19, of which 17 were waited for; matrix products, arithmetic and copies ran while one was open for 7% of the time, Pallas kernels for 0%

commit v1 on v0

v1 whole, which is shorter than its diff:
```python
import functools
import math

import jax
import jax.numpy as jnp
from jax import lax
from jax.experimental import pallas as pl
from jax.experimental.pallas import tpu as pltpu
from jax.sharding import PartitionSpec as P

HEADS = 4
HEAD = 256


EPS = 1e-06
GELU_C = math.sqrt(2.0 / math.pi)
NEG_FILL = -1e30


def inverse_rms(values):
    return lax.rsqrt(jnp.mean(values * values, axis=-1, keepdims=True) + EPS)


def norm_back(values, scale_inv, gain, grad_out):
    weighted = grad_out * gain
    cubed = scale_inv * scale_inv * scale_inv
    return scale_inv * weighted - values * cubed * jnp.mean(
        weighted * values, axis=-1, keepdims=True
    )


def gelu_pair(values):
    inner = GELU_C * (values + 0.044715 * values * values * values)
    tanh_val = jnp.tanh(inner)
    result = 0.5 * values * (1.0 + tanh_val)
    slope = 0.5 * (1.0 + tanh_val) + 0.5 * values * (1.0 - tanh_val * tanh_val) * GELU_C * (
        1.0 + 3.0 * 0.044715 * values * values
    )
    return (result, slope)


def rotate(values, cosine, sine):
    middle = values.shape[-1] // 2
    first = values[..., :middle]
    second = values[..., middle:]
    return jnp.concatenate(
        [first * cosine - second * sine, second * cosine + first * sine], axis=-1
    )


def unrotate(grads, cosine, sine):
    middle = grads.shape[-1] // 2
    first = grads[..., :middle]
    second = grads[..., middle:]
    return jnp.concatenate(
        [first * cosine + second * sine, second * cosine - first * sine], axis=-1
    )


def rope_tables(positions):
    middle = HEAD // 2
    freqs = jnp.exp(-(2.0 * jnp.arange(middle, dtype=jnp.float32) / HEAD) * math.log(1000000.0))
    angles = positions[:, None] * freqs[None, :]
    return (jnp.cos(angles), jnp.sin(angles))


def matmul(left, right):
    return jnp.dot(left, right, preferred_element_type=jnp.float32)


def matmul_tn(left, right):
    return lax.dot_general(
        left, right, (((0,), (0,)), ((), ())), preferred_element_type=jnp.float32
    )


def matmul_nt(left, right):
    return lax.dot_general(
        left, right, (((1,), (1,)), ((), ())), preferred_element_type=jnp.float32
    )


MESH = pl.DeviceIdType.MESH


def swap_kernel(size, axis, kinds, *refs):
    count = len(kinds)
    ins, outs = refs[:count], refs[count : 2 * count]
    send, recv, local = refs[2 * count :]
    me = lax.axis_index(axis)
    barrier = pltpu.get_barrier_semaphore()
    for step in range(1, size):
        peer = lax.rem(me + step, size)
        pl.semaphore_signal(barrier, inc=1, device_id={axis: peer}, device_id_type=MESH)
    pl.semaphore_wait(barrier, size - 1)
    copies = []
    for item, kind in enumerate(kinds):
        for step in range(1, size):
            peer = lax.rem(me + step, size)
            source = ins[item].at[peer] if kind == "swap" else ins[item]
            copy = pltpu.make_async_remote_copy(
                src_ref=source,
                dst_ref=outs[item].at[me],
                send_sem=send.at[item, step - 1],
                recv_sem=recv.at[item, step - 1],
                device_id={axis: peer},
                device_id_type=MESH,
            )
            copy.start()
            copies.append(copy)
    for item, kind in enumerate(kinds):
        source = ins[item].at[me] if kind == "swap" else ins[item]
        copy = pltpu.make_async_copy(source, outs[item].at[me], local.at[item])
        copy.start()
        copies.append(copy)
    for copy in copies:
        copy.wait()


def pair_gather_kernel(size, axis, kinds, *refs):
    count = len(kinds)
    ins, outs = refs[:count], refs[count : 2 * count]
    send, recv, pass_send, pass_recv, local = refs[2 * count :]
    me = lax.axis_index(axis)
    twin = me + 1 - 2 * lax.rem(me, 2)
    half = size // 2
    barrier = pltpu.get_barrier_semaphore()
    for step in range(1, half):
        peer = lax.rem(me + 2 * step, size)
        pl.semaphore_signal(barrier, inc=1, device_id={axis: peer}, device_id_type=MESH)
    pl.semaphore_signal(barrier, inc=1, device_id={axis: twin}, device_id_type=MESH)
    pl.semaphore_wait(barrier, half)
    copies, last = [], []
    for item in range(count):
        row = []
        for step in range(1, half):
            peer = lax.rem(me + 2 * step, size)
            copy = pltpu.make_async_remote_copy(
                src_ref=ins[item],
                dst_ref=outs[item].at[me],
                send_sem=send.at[item, step],
                recv_sem=recv.at[item, step],
                device_id={axis: peer},
                device_id_type=MESH,
            )
            copy.start()
            row.append(copy)
        copies.append(row)
    for item in range(count):
        copy = pltpu.make_async_remote_copy(
            src_ref=ins[item],
            dst_ref=outs[item].at[me],
            send_sem=pass_send.at[item, 0],
            recv_sem=pass_recv.at[item, 0],
            device_id={axis: twin},
            device_id_type=MESH,
        )
        copy.start()
        last.append(copy)
        copy = pltpu.make_async_copy(ins[item], outs[item].at[me], local.at[item])
        copy.start()
        last.append(copy)
    for item in range(count):
        for step in range(1, half):
            copies[item][step - 1].wait_recv()
            origin = lax.rem(me + size - 2 * step, size)
            copy = pltpu.make_async_remote_copy(
                src_ref=outs[item].at[origin],
                dst_ref=outs[item].at[origin],
                send_sem=pass_send.at[item, step],
                recv_sem=pass_recv.at[item, step],
                device_id={axis: twin},
                device_id_type=MESH,
            )
            copy.start()
            last.append(copy)
    for row in copies:
        for copy in row:
            copy.wait_send()
    for copy in last:
        copy.wait()


def exchange(arrays, kinds, axis, size, ident):
    count = len(arrays)
    pairs = all(kind == "gather" for kind in kinds) and axis == "ctx" and size % 2 == 0
    shapes = tuple(
        jax.ShapeDtypeStruct(x.shape if kind == "swap" else (size,) + x.shape, x.dtype)
        for x, kind in zip(arrays, kinds)
    )
    dma = pltpu.SemaphoreType.DMA
    if pairs:
        half = size // 2
        scratch = [dma((count, half))] * 4 + [dma((count,))]
        body = pair_gather_kernel
    else:
        scratch = [dma((count, size - 1))] * 2 + [dma((count,))]
        body = swap_kernel
    moved = sum(x.size * x.dtype.itemsize for x in shapes)
    return pl.pallas_call(
        functools.partial(body, size, axis, tuple(kinds)),
        out_shape=shapes,
        in_specs=[pl.BlockSpec(memory_space=pl.ANY)] * count,
        out_specs=tuple(pl.BlockSpec(memory_space=pl.ANY) for _ in arrays),
        scratch_shapes=scratch,
        compiler_params=pltpu.CompilerParams(collective_id=ident, has_side_effects=True),
        cost_estimate=pl.CostEstimate(flops=0, bytes_accessed=20 * moved, transcendentals=0),
        name=f"exchange_{ident}",
    )(*arrays)


def by_columns(array, parts):
    rows, columns = array.shape
    return jnp.transpose(array.reshape(rows, parts, columns // parts), (1, 0, 2))


def from_columns(array):
    parts, rows, columns = array.shape
    return jnp.transpose(array, (1, 0, 2)).reshape(rows, parts * columns)


def sum_blocks(array):
    return jnp.sum(array.astype(jnp.float32), axis=0)


def on_device(
    dp,
    ctx,
    tokens,
    in_gain,
    query_weight,
    key_weight,
    value_weight,
    query_gain,
    key_gain,
    out_weight,
    attn_post_gain,
    ffn_pre_gain,
    gate_weight,
    up_weight,
    down_weight,
    ffn_post_gain,
    cotangent,
):
    rows, width = tokens.shape
    bf16 = jnp.bfloat16
    scaling = 1.0 / math.sqrt(HEAD)
    ctx_index = lax.axis_index("ctx")
    query_pos = ctx_index * rows + jnp.arange(rows, dtype=jnp.int32)
    cosine, sine = rope_tables(query_pos.astype(jnp.float32))
    gate_full, up_full, down_full = (
        lax.all_gather(gate_weight, "dp", axis=0, tiled=True),
        lax.all_gather(up_weight, "dp", axis=0, tiled=True),
        lax.all_gather(down_weight, "dp", axis=0, tiled=True),
    )

    mixed = jnp.concatenate([query_weight, key_weight, value_weight], axis=1)
    mixed_columns = mixed.shape[1] // ctx
    out_columns = out_weight.shape[1] // ctx
    mixed_slice = lax.dynamic_slice_in_dim(mixed, ctx_index * mixed_columns, mixed_columns, 1)
    out_slice = lax.dynamic_slice_in_dim(out_weight, ctx_index * out_columns, out_columns, 1)
    gains = (in_gain, query_gain, key_gain, attn_post_gain, ffn_pre_gain, ffn_post_gain)
    cuts = [0]
    for gain in gains:
        cuts.append(cuts[-1] + gain.shape[0])
    packed_gains = jnp.concatenate([gain.astype(jnp.float32) for gain in gains])[None]
    mixed_dp, out_dp, gains_dp = exchange(
        (mixed_slice, out_slice, packed_gains), ("gather",) * 3, "dp", dp, 0
    )
    gains_dp = gains_dp[:, 0]
    gain_in, gain_query, gain_key, gain_attn, gain_pre, gain_post = (
        gains_dp[:, low:high].reshape(-1) for low, high in zip(cuts[:-1], cuts[1:])
    )
    mixed_all, out_all, tokens_all = exchange(
        (
            mixed_dp.reshape(-1, mixed_columns),
            out_dp.reshape(-1, out_columns),
            tokens,
        ),
        ("gather",) * 3,
        "ctx",
        ctx,
        1,
    )
    mixed_full = from_columns(mixed_all)
    out_full = from_columns(out_all)
    qwidth = query_weight.shape[1]
    kwidth = key_weight.shape[1]
    query_full = mixed_full[:, :qwidth]
    key_full = mixed_full[:, qwidth : qwidth + kwidth]
    value_full = mixed_full[:, qwidth + kwidth :]

    inputs_f = tokens.astype(jnp.float32)
    inv_one = inverse_rms(inputs_f)
    normed_one = (inputs_f * inv_one * gain_in).astype(bf16)
    all_f = tokens_all.reshape(-1, width).astype(jnp.float32)
    normed_all = (all_f * inverse_rms(all_f) * gain_in).astype(bf16)
    key_pos = jnp.arange(all_f.shape[0], dtype=jnp.int32)
    cosine_all, sine_all = rope_tables(key_pos.astype(jnp.float32))
    queries = matmul(normed_one, query_full).reshape(rows, HEADS, HEAD)
    keys = matmul(normed_one, key_full)
    keys_every = matmul(normed_all, key_full)
    value_all = matmul(normed_all, value_full).astype(bf16)
    inv_query = inverse_rms(queries)
    inv_key = inverse_rms(keys)
    query_rot = (
        rotate(queries * inv_query * gain_query, cosine[:, None, :], sine[:, None, :]) * scaling
    ).astype(bf16)
    key_all = rotate(
        keys_every * inverse_rms(keys_every) * gain_key, cosine_all, sine_all
    ).astype(bf16)
    allowed = (query_pos[:, None] >= key_pos[None, :])[None]
    scores = jnp.einsum("qhd,kd->hqk", query_rot, key_all, preferred_element_type=jnp.float32)
    scores = jnp.where(allowed, scores, NEG_FILL)
    row_max = jnp.max(scores, axis=-1, keepdims=True)
    weights = jnp.where(allowed, jnp.exp(scores - row_max), 0.0)
    total = jnp.sum(weights, axis=-1, keepdims=True)
    accum = jnp.einsum(
        "hqk,kd->hqd", weights.astype(bf16), value_all, preferred_element_type=jnp.float32
    )
    log_total = row_max + jnp.log(total)
    attn_heads = jnp.transpose(accum / total, (1, 0, 2)).astype(bf16)
    attn_out = attn_heads.reshape(rows, HEADS * HEAD)
    projected = matmul(attn_out, out_full)
    inv_proj = inverse_rms(projected)
    residual = inputs_f + projected * inv_proj * gain_attn
    inv_two = inverse_rms(residual)
    normed_two = (residual * inv_two * gain_pre).astype(bf16)

    (rows_all,) = exchange((normed_two,), ("gather",), "ctx", ctx, 2)
    rows_all = rows_all.reshape(-1, width)
    gate = matmul(rows_all, gate_full)
    upper = matmul(rows_all, up_full)
    gelu_val, gelu_der = gelu_pair(gate)
    hidden = (gelu_val * upper).astype(bf16)
    ffn_part = matmul_nt(hidden, down_full).astype(bf16).reshape(ctx, rows, width)
    (ffn_parts,) = exchange((ffn_part,), ("swap",), "ctx", ctx, 3)
    ffn_sum = sum_blocks(ffn_parts)
    inv_ffn = inverse_rms(ffn_sum)
    block_out = (residual + ffn_sum * inv_ffn * gain_post).astype(bf16)
    cot = cotangent.astype(jnp.float32)
    grad_post = jnp.sum(cot * ffn_sum * inv_ffn, axis=0)
    ffn_sum_grad = norm_back(ffn_sum, inv_ffn, gain_post, cot).astype(bf16)

    (grad_all,) = exchange((ffn_sum_grad,), ("gather",), "ctx", ctx, 4)
    grad_all = grad_all.reshape(-1, width)
    down_shard = lax.psum_scatter(
        matmul_tn(grad_all, hidden).astype(bf16), "dp", scatter_dimension=0, tiled=True
    ).astype(jnp.float32)
    hidden_grad = matmul(grad_all, down_full)
    gate_grad = (hidden_grad * upper * gelu_der).astype(bf16)
    up_grad = (hidden_grad * gelu_val).astype(bf16)
    gate_shard = lax.psum_scatter(
        matmul_tn(rows_all, gate_grad).astype(bf16), "dp", scatter_dimension=0, tiled=True
    ).astype(jnp.float32)
    up_shard = lax.psum_scatter(
        matmul_tn(rows_all, up_grad).astype(bf16), "dp", scatter_dimension=0, tiled=True
    ).astype(jnp.float32)
    two_part = (matmul_nt(gate_grad, gate_full) + matmul_nt(up_grad, up_full)).astype(bf16)
    two_parts, attn_all = exchange(
        (two_part.reshape(ctx, rows, width), attn_out), ("swap", "gather"), "ctx", ctx, 5
    )
    normed_two_grad = sum_blocks(two_parts)
    attn_all = attn_all.reshape(-1, attn_out.shape[1])
    grad_pre = jnp.sum(normed_two_grad * residual * inv_two, axis=0)
    residual_grad = cot + norm_back(residual, inv_two, gain_pre, normed_two_grad)
    grad_attn = jnp.sum(residual_grad * projected * inv_proj, axis=0)
    projected_grad = norm_back(projected, inv_proj, gain_attn, residual_grad).astype(bf16)
    attn_out_grad = matmul_nt(projected_grad, out_full).astype(bf16).reshape(rows, HEADS, HEAD)
    delta = jnp.sum(attn_out_grad.astype(jnp.float32) * attn_heads.astype(jnp.float32), axis=-1)
    delta = jnp.transpose(delta, (1, 0))[:, :, None]
    probs = jnp.where(allowed, jnp.exp(scores - log_total), 0.0)
    prob_grad = jnp.einsum(
        "qhd,kd->hqk", attn_out_grad, value_all, preferred_element_type=jnp.float32
    )
    score_grad = (probs * (prob_grad - delta)).astype(bf16)
    values_part = jnp.einsum(
        "hqk,qhd->kd", probs.astype(bf16), attn_out_grad, preferred_element_type=jnp.float32
    )
    keys_part = jnp.einsum("hqk,qhd->kd", score_grad, query_rot, preferred_element_type=jnp.float32)
    query_rot_grad = jnp.einsum(
        "hqk,kd->qhd", score_grad, key_all, preferred_element_type=jnp.float32
    )
    keys_parts, values_parts = exchange(
        (
            keys_part.astype(bf16).reshape(ctx, rows, kwidth),
            values_part.astype(bf16).reshape(ctx, rows, kwidth),
        ),
        ("swap", "swap"),
        "ctx",
        ctx,
        6,
    )
    key_rot_grad = sum_blocks(keys_parts)
    value_grad = sum_blocks(values_parts).astype(bf16)
    query_normed_grad = unrotate(query_rot_grad * scaling, cosine[:, None, :], sine[:, None, :])
    grad_qgain = jnp.sum(query_normed_grad * queries * inv_query, axis=(0, 1))
    query_grad = (
        norm_back(queries, inv_query, gain_query, query_normed_grad)
        .reshape(rows, HEADS * HEAD)
        .astype(bf16)
    )
    key_normed_grad = unrotate(key_rot_grad, cosine, sine)
    grad_kgain = jnp.sum(key_normed_grad * keys * inv_key, axis=0)
    key_grad = norm_back(keys, inv_key, gain_key, key_normed_grad).astype(bf16)
    mixed_grad = jnp.concatenate([query_grad, key_grad, value_grad], axis=1)
    normed_one_grad = matmul_nt(mixed_grad, mixed_full)
    grad_in = jnp.sum(normed_one_grad * inputs_f * inv_one, axis=0)
    input_grad = residual_grad + norm_back(inputs_f, inv_one, gain_in, normed_one_grad)

    gain_grads = (grad_in, grad_qgain, grad_kgain, grad_attn, grad_pre, grad_post)
    packed = jnp.concatenate([grad.reshape(dp, -1) for grad in gain_grads], axis=1)
    mixed_cols, out_cols, gain_parts = exchange(
        (by_columns(mixed_grad, ctx), by_columns(projected_grad, ctx), by_columns(packed, ctx)),
        ("swap",) * 3,
        "ctx",
        ctx,
        7,
    )
    mixed_w = matmul_tn(normed_all, mixed_cols.reshape(-1, mixed_columns)).astype(bf16)
    out_w = matmul_tn(attn_all, out_cols.reshape(-1, out_columns)).astype(bf16)
    mixed_w, out_w, gain_parts = exchange(
        (
            mixed_w.reshape(dp, -1, mixed_columns),
            out_w.reshape(dp, -1, out_columns),
            sum_blocks(gain_parts)[:, None],
        ),
        ("swap",) * 3,
        "dp",
        dp,
        8,
    )
    mixed_w, out_w, gain_parts = exchange(
        (sum_blocks(mixed_w).astype(bf16), sum_blocks(out_w).astype(bf16), sum_blocks(gain_parts)),
        ("gather",) * 3,
        "ctx",
        ctx,
        9,
    )
    mixed_w = from_columns(mixed_w).astype(jnp.float32)
    out_w = from_columns(out_w).astype(jnp.float32)
    gain_done = gain_parts.reshape(-1)
    share = [gain_done[low:high] for low, high in zip(cuts[:-1], cuts[1:])]
    return (
        block_out,
        input_grad,
        share[0],
        mixed_w[:, :qwidth],
        mixed_w[:, qwidth : qwidth + kwidth],
        mixed_w[:, qwidth + kwidth :],
        share[1],
        share[2],
        out_w,
        share[3],
        share[4],
        gate_shard,
        up_shard,
        down_shard,
        share[5],
    )


def solution(mesh):
    return jax.shard_map(
        functools.partial(on_device, mesh.shape["dp"], mesh.shape["ctx"]),
        mesh=mesh,
        in_specs=(
            P(("dp", "ctx"), None),
            P("dp"),
            P("dp", None),
            P("dp", None),
            P("dp", None),
            P("dp"),
            P("dp"),
            P("dp", None),
            P("dp"),
            P("dp"),
            P("dp", "ctx"),
            P("dp", "ctx"),
            P("dp", "ctx"),
            P("dp"),
            P(("dp", "ctx"), None),
        ),
        out_specs=(
            P(("dp", "ctx"), None),
            P(("dp", "ctx"), None),
            P("dp"),
            P("dp", None),
            P("dp", None),
            P("dp", None),
            P("dp"),
            P("dp"),
            P("dp", None),
            P("dp"),
            P("dp"),
            P("dp", "ctx"),
            P("dp", "ctx"),
            P("dp", "ctx"),
            P("dp"),
        ),
        check_vma=False,
    )
```

time: 1120 us -> 538 us (0.48)
  waiting for transfers between devices: 834 us -> 2.12 us
  Pallas kernels: 0 us -> 329 us
  blocking collectives: 121 us -> 0 us
  local copies, waits for them, and re-layouts: 24.7 us -> 53.7 us
  other arithmetic: 23.1 us -> 47.9 us
    reduce_scatter x11 -> x3, waiting for transfers between devices: 571 us -> 0.01 us  [the longest x1 0.01 us: on_device(): lax.psum_scatter(matmul_tn(grad_all, hidden).astype(bf16), 'dp', scatter_...]
    pallas_call x0 -> x10, Pallas kernels: none -> 329 us  [exchange(): pl.pallas_call(functools.partial(body, size, axis, tuple(kinds)), out_sha...]
    all_gather x7 -> x3, waiting for transfers between devices: 188 us -> 0.01 us  [the longest x1 0.01 us: on_device(): lax.all_gather(gate_weight, 'dp', axis=0, tiled=True)]
    psum x1 -> x0, waiting for transfers between devices: 71.9 us -> none  [on_device(): lax.psum((share_in, share_query, share_key, share_value, share_qgain, sha...]
    all_gather x4 -> x0, blocking collectives: 64.7 us -> none  [the longest x1 22.8 us: gather_attention(): lax.all_gather(key_weight, 'dp', axis=0, tiled=True)]
    unnamed x2 -> x0, blocking collectives: 43.1 us -> none
    psum x1 -> x0, blocking collectives: 12.9 us -> none  [on_device(): lax.psum((share_in, share_query, share_key, share_value, share_qgain, sha...]
    reduce_sum x1 -> x9, other arithmetic: 0.46 us -> 12.6 us  [the longest x8 12.1 us: sum_blocks(): return jnp.sum(array.astype(jnp.float32), axis=0)]
  transfers between devices with their start and end apart: 19 -> 6, of which waited for: 17 -> 0; matrix products, arithmetic and copies ran while one was open for 7% -> 31% of each run, Pallas kernels for 0% -> 53%
where the time goes in v1:
time: 538 us; the launch traced here: 531 us
  Pallas kernels  329 us (61%)
  matrix products  81.8 us (15%)
  local copies, waits for them, and re-layouts  53.7 us (10%)
  other arithmetic  47.9 us (9%)
  between operations  15.6 us (3%)
    pallas_call x10, Pallas kernels, exchange(): pl.pallas_call(functools.partial(body, size, axis, tuple(kinds)), out_sha...  329 us
    dot_general x8, matrix products, matmul(): return jnp.dot(left, right, preferred_element_type=jnp.float32)  35.4 us
    dot_general x5, matrix products, matmul_tn(): lax.dot_general(left, right, (((0,), (0,)), ((), ())), preferred_element_...  20.5 us
    dot_general x5, matrix products, matmul_nt(): lax.dot_general(left, right, (((1,), (1,)), ((), ())), preferred_element_...  18.7 us
    reduce_sum x8, other arithmetic, sum_blocks(): return jnp.sum(array.astype(jnp.float32), axis=0)  12.1 us
    transpose x2, local copies, waits for them, and re-layouts, from_columns(): return jnp.transpose(array, (1, 0, 2)).reshape(rows, parts * columns)  11.9 us
  transfers between devices with their start and end apart: 6, of which 0 were waited for; matrix products, arithmetic and copies ran while one was open for 31% of the time, Pallas kernels for 53%

profile of v1, /device:TPU:0, one launch (start us, length us, event | category | flops | bytes accessed | tf_op | source)
XLA Modules:
  0.0 530.7 jit_solution(16293064875747760551)
XLA Ops:
  9.5 4.2 concatenate.29
  15.0 1.8 fusion.73.refs_0_
  16.9 59.4 %exchange_0.1 = (bf16[4,288,192]{2,1,0:T(8,128)(2,1)}, bf16[4,256,144]{2,1,0:T(8,128)(2,1)}, f32[4,1,1280]{2,1,0:T(1,128)}) custom-call(bf16[288,192]{1,0:T(8,128)(2,1)} %fusion.73.refs_0_, bf16[256,144]{1,0:T(8,128)(2,1)} %constant_dynamic-slice_fusion.refs_1_, f32[1,1280]{1,0:T(1,128)} %reshape.397.refs_2_), custom_call_target="tpu_custom_call" | custom-call | bytes 15155200 | tf_op jit(solution)/shard_map/exchange_0/pallas_call | solution.py:200
  77.9 66.6 %exchange_1.1 = (bf16[8,1152,192]{2,1,0:T(8,128)(2,1)}, bf16[8,1024,144]{2,1,0:T(8,128)(2,1)}, bf16[8,128,1152]{2,1,0:T(8,128)(2,1)}) custom-call(bf16[1152,192]{1,0:T(8,128)(2,1)} %bitcast.193, bf16[1024,144]{1,0:T(8,128)(2,1)} %bitcast.196, bf16[128,1152]{1,0:T(8,128)(2,1)} %refs_2_.1), custom_call_target="tpu_custom_call" | custom-call | bytes 165150720 | tf_op jit(solution)/shard_map/exchange_1/pallas_call | solution.py:200
  144.5 2.2 multiply_reduce_fusion
  147.4 6.6 %copy.162 = bf16[1152,8,192]{0,2,1:T(8,128)(2,1)} copy(bf16[1152,8,192]{2,0,1:T(8,128)(2,1)} %bitcast.159) | data formatting | bytes 7077888 | tf_op jit(solution)/shard_map/transpose | solution.py:219
  154.7 2.0 multiply_reduce_fusion.1
  156.7 2.0 fusion.25
  159.3 2.6 fusion.10
  164.6 2.3 fusion.60
  169.2 5.3 copy.168
  179.4 18.6 %exchange_2.1 = bf16[8,128,1152]{2,1,0:T(8,128)(2,1)} custom-call(bf16[128,1152]{1,0:T(8,128)(2,1)} %multiply_convert_fusion.4.refs_0_), custom_call_target="tpu_custom_call" | custom-call | bytes 47185920 | tf_op jit(solution)/shard_map/exchange_2/pallas_call | solution.py:200
  207.2 2.7 multiply_reduce_fusion.14
  209.9 6.5 %fusion.96 = f32[1024,864]{0,1:T(8,128)} fusion(bf16[1024,1152]{1,0:T(8,128)(2,1)} %bitcast.167, bf16[1152,864]{1,0:T(8,128)(2,1)} %all-gather.4.cloned.1.call-done), kind=kOutput, calls=%fused_computation.198 | convolution fusion | flops 2038431744 | bytes 7888896 | tf_op jit(solution)/shard_map/dot_general | solution.py:68
  216.4 9.0 %multiply_convert_fusion.2 = (bf16[1024,864]{0,1:T(8,128)(2,1)}, f32[1024,864]{0,1:T(8,128)}) fusion(f32[1024,864]{0,1:T(8,128)} %fusion.96, bf16[1024,1152]{1,0:T(8,128)(2,1)} %bitcast.168, bf16[1152,864]{1,0:T(8,128)(2,1)} %all-gather.6.cloned.1.call-done), kind=kOutput, calls=%fused_computation.22 | convolution fusion | flops 2047279104 | bytes 13197312 | tf_op jit(solution)/shard_map/dot_general | solution.py:68
  225.4 6.4 %convolution_convert_fusion = bf16[1024,1152]{1,0:T(8,128)(2,1)} fusion(bf16[1024,864]{0,1:T(8,128)(2,1)} %get-tuple-element.193, bf16[1152,864]{1,0:T(8,128)(2,1)} %all-gather.8.cloned.1.call-done), kind=kOutput, calls=%fused_computation.10 | convolution fusion | flops 2039611392 | bytes 6119424 | tf_op jit(solution)/shard_map/dot_general | solution.py:78
  231.8 28.1 %exchange_3.1 = bf16[8,128,1152]{2,1,0:T(8,128)(2,1)} custom-call(bf16[8,128,1152]{2,1,0:T(8,128)(2,1)} %bitcast.173), custom_call_target="tpu_custom_call" | custom-call | bytes 47185920 | tf_op jit(solution)/shard_map/exchange_3/pallas_call | solution.py:200
  260.0 2.1 convert_reduce_fusion.1
  264.1 18.9 %exchange_4.1 = bf16[8,128,1152]{2,1,0:T(8,128)(2,1)} custom-call(bf16[128,1152]{1,0:T(8,128)(2,1)} %get-tuple-element.153.refs_0_), custom_call_target="tpu_custom_call" | custom-call | bytes 47185920 | tf_op jit(solution)/shard_map/exchange_4/pallas_call | solution.py:200
  283.0 6.6 %convolution_convert_fusion.1 = bf16[1152,864]{1,0:T(8,128)(2,1)} fusion(bf16[1024,1152]{1,0:T(8,128)(2,1)} %bitcast.171, bf16[1024,864]{0,1:T(8,128)(2,1)} %get-tuple-element.193), kind=kOutput, calls=%fused_computation.11 | convolution fusion | flops 2039427072 | bytes 6119424 | tf_op jit(solution)/shard_map/dot_general | solution.py:72
  290.9 9.7 %multiply_convert_fusion.1 = (bf16[1024,864]{0,1:T(8,128)(2,1)S(1)}, bf16[1024,864]{0,1:T(8,128)(2,1)S(1)}) fusion(f32[1024,864]{0,1:T(8,128)} %fusion.96, f32[1024,864]{0,1:T(8,128)} %get-tuple-element.194, bf16[1024,1152]{1,0:T(8,128)(2,1)} %bitcast.172, bf16[1152,864]{1,0:T(8,128)(2,1)} %all-gather.8.cloned.1.call-done), kind=kOutput, calls=%fused_computation.21 | convolution fusion | flops 2058780672 | bytes 14966784 | tf_op jit(solution)/shard_map/dot_general | solution.py:68
  300.6 2.9 fusion.97
  303.6 4.3 add_convert_fusion
  307.9 49.8 %exchange_5.1 = (bf16[8,128,1152]{2,1,0:T(8,128)(2,1)}, bf16[8,128,1024]{2,1,0:T(8,128)(2,1)}) custom-call(bf16[8,128,1152]{2,1,0:T(8,128)(2,1)} %bitcast.166, bf16[128,1024]{1,0:T(8,128)(2,1)} %bitcast.176), custom_call_target="tpu_custom_call" | custom-call | bytes 89128960 | tf_op jit(solution)/shard_map/exchange_5/pallas_call | solution.py:200
  357.8 2.2 convert_reduce_fusion
  360.7 1.8 multiply_reduce_fusion.3
  362.5 4.1 convolution_convert_fusion.3
  368.6 1.9 copy.182
  372.5 2.7 fusion.16
  381.1 15.8 %exchange_6.1 = (bf16[8,128,256]{2,1,0:T(8,128)(2,1)}, bf16[8,128,256]{2,1,0:T(8,128)(2,1)}) custom-call(bf16[8,128,256]{2,1,0:T(8,128)(2,1)} %bitcast.194, bf16[8,128,256]{2,1,0:T(8,128)(2,1)} %bitcast.195), custom_call_target="tpu_custom_call" | custom-call | bytes 20971520 | tf_op jit(solution)/shard_map/exchange_6/pallas_call | solution.py:200
  396.9 1.8 reduce_sum.306
  400.8 5.5 %convolution_convert_fusion.2 = bf16[1152,864]{1,0:T(8,128)(2,1)} fusion(bf16[1024,1152]{1,0:T(8,128)(2,1)S(1)} %bitcast.170, bf16[1024,864]{0,1:T(8,128)(2,1)} %copy-done.81), kind=kOutput, calls=%fused_computation.12 | convolution fusion | flops 2039427072 | bytes 6119424 | tf_op jit(solution)/shard_map/dot_general | solution.py:72
  409.9 3.6 fusion.57
  417.1 16.8 %exchange_7.1 = (bf16[8,128,192]{2,1,0:T(8,128)(2,1)}, bf16[8,128,144]{2,1,0:T(8,128)(2,1)}, f32[8,4,160]{2,1,0:T(4,128)}) custom-call(bf16[8,128,192]{2,1,0:T(8,128)(2,1)} %bitcast.177, bf16[8,128,144]{2,1,0:T(8,128)(2,1)} %bitcast.179, f32[8,4,160]{2,1,0:T(4,128)} %bitcast.197), custom_call_target="tpu_custom_call" | custom-call | bytes 14172160 | tf_op jit(solution)/shard_map/exchange_7/pallas_call | solution.py:200
  433.9 2.4 fusion.26
  437.3 1.9 fusion.9
  440.9 37.1 %exchange_8.1 = (bf16[4,288,192]{2,1,0:T(8,128)(2,1)}, bf16[4,256,144]{2,1,0:T(8,128)(2,1)}, f32[4,1,160]{2,1,0:T(1,128)}) custom-call(bf16[4,288,192]{2,1,0:T(8,128)(2,1)} %bitcast.174, bf16[4,256,144]{2,1,0:T(8,128)(2,1)} %bitcast.178, f32[4,1,160]{2,1,0:T(1,128)} %broadcast_in_dim.33.refs_2_), custom_call_target="tpu_custom_call" | custom-call | bytes 14796800 | tf_op jit(solution)/shard_map/exchange_8/pallas_call | solution.py:200
  478.0 1.9 reduce_sum.317.refs_0_
  479.9 1.8 reduce_sum.318.refs_1_
  483.0 18.1 %exchange_9.1 = (bf16[8,288,192]{2,1,0:T(8,128)(2,1)}, bf16[8,256,144]{2,1,0:T(8,128)(2,1)}, f32[8,1,160]{2,1,0:T(1,128)}) custom-call(bf16[288,192]{1,0:T(8,128)(2,1)} %reduce_sum.317.refs_0_, bf16[256,144]{1,0:T(8,128)(2,1)} %reduce_sum.318.refs_1_, f32[1,160]{1,0:T(1,128)} %bitcast.202), custom_call_target="tpu_custom_call" | custom-call | bytes 29593600 | tf_op jit(solution)/shard_map/exchange_9/pallas_call | solution.py:200
  503.9 2.0 reshape.399
  506.0 2.5 slice.122
  508.7 1.6 copy.190
  510.3 2.7 copy.191
  514.4 1.9 fusion.91
  517.4 2.1 convert_element_type.223
  519.5 2.1 convert_element_type.219
  521.5 2.1 convert_element_type.221
  (287 shorter events, 58.2 us)
Async XLA Ops:
  7.2 7.1 %copy-start = (bf16[256,1152]{1,0:T(8,128)(2,1)S(1)}, bf16[256,1152]{1,0:T(8,128)(2,1)}, u32[]{:S(2)}) copy-start(bf16[256,1152]{1,0:T(8,128)(2,1)} %param.22) | copy-start | bytes 1769476
  7.2 70.6 %copy-start.7 = (bf16[128,1152]{1,0:T(8,128)(2,1)S(1)}, bf16[128,1152]{1,0:T(8,128)(2,1)}, u32[]{:S(2)}) copy-start(bf16[128,1152]{1,0:T(8,128)(2,1)} %refs_2_.1) | copy-start | bytes 884740
  7.2 202.7 %all-gather.4.cloned.1.call-start = ((), (), s32[]{:S(2)}) async-start(), calls=%async_computation.3 | async-start | bytes 2580480 | tf_op jit(solution)/shard_map/all_gather | solution.py:252
  7.9 208.5 %all-gather.6.cloned.1.call-start = ((), (), s32[]{:S(2)}) async-start(), calls=%async_computation.4 | async-start | bytes 2580480 | tf_op jit(solution)/shard_map/all_gather | solution.py:253
  8.7 216.7 %all-gather.8.cloned.1.call-start = ((), (), s32[]{:S(2)}) async-start(), calls=%async_computation.5 | async-start | bytes 2580480 | tf_op jit(solution)/shard_map/all_gather | solution.py:254
  9.4 508.0 %reduce-scatter.8.cloned.1.call-start = ((), (), s32[]{:S(2)}) async-start(), calls=%async_computation.8 | async-start | bytes 2580480 | tf_op jit(solution)/shard_map/reduce_scatter | solution.py:347
  77.8 86.8 %copy-start.61 = (f32[128]{0:T(128)}, f32[128]{0:T(128)S(1)}, u32[]{:S(2)}) copy-start(f32[128]{0:T(128)S(1)} %multiply_exponential_fusion) | copy-start | bytes 1540
  147.4 11.9 %copy-start.43 = (f32[1152]{0:T(1024)}, f32[1152]{0:T(1024)S(1)}, u32[]{:S(2)}) copy-start(f32[1152]{0:T(1024)S(1)} %mul.753) | copy-start | bytes 13828
  147.4 6.7 %copy-start.2 = (bf16[8,128,1152]{2,1,0:T(8,128)(2,1)S(1)}, bf16[8,128,1152]{2,1,0:T(8,128)(2,1)}, u32[]{:S(2)}) copy-start(bf16[8,128,1152]{2,1,0:T(8,128)(2,1)} %get-tuple-element.36) | copy-start | bytes 7077892
  158.6 9.6 %copy-start.78 = (bf16[1024,256,1]{1,0,2:T(8,128)(2,1)}, bf16[1024,256,1]{1,0,2:T(8,128)(2,1)S(1)}, u32[]{:S(2)}) copy-start(bf16[1024,256,1]{1,0,2:T(8,128)(2,1)S(1)} %fusion.25) | copy-start | bytes 1572868
  158.8 5.6 %copy-start.51 = (f32[256]{0:T(256)}, f32[256]{0:T(256)S(1)}, u32[]{:S(2)}) copy-start(f32[256]{0:T(256)S(1)} %mul.759) | copy-start | bytes 3076
  161.9 5.0 copy-start.4
  163.2 3.9 copy-start.54
  163.2 3.9 copy-start.66
  163.3 5.0 copy-start.31
  169.1 5.4 %copy-start.23 = (bf16[128,4,256]{2,0,1:T(8,128)(2,1)}, bf16[128,4,256]{2,0,1:T(8,128)(2,1)S(1)}, u32[]{:S(2)}) copy-start(bf16[128,4,256]{2,0,1:T(8,128)(2,1)S(1)} %fusion.27) | copy-start | bytes 786436
  169.1 5.3 %copy-start.15 = (bf16[4,16,8,256]{3,2,0,1:T(8,128)(2,1)}, bf16[4,16,8,256]{3,2,0,1:T(8,128)(2,1)S(1)}, u32[]{:S(2)}) copy-start(bf16[4,16,8,256]{3,2,0,1:T(8,128)(2,1)S(1)} %copy.206) | copy-start | bytes 786436
  289.6 229.9 %reduce-scatter.4.cloned.1.call-start = ((), (), s32[]{:S(2)}) async-start(), calls=%async_computation.6 | async-start | bytes 2580480 | tf_op jit(solution)/shard_map/reduce_scatter | solution.py:353
  290.9 9.7 %copy-start.76 = (bf16[1152,864]{1,0:T(8,128)(2,1)S(1)}, bf16[1152,864]{1,0:T(8,128)(2,1)}, u32[]{:S(2)}) copy-start(bf16[1152,864]{1,0:T(8,128)(2,1)} %all-gather.4.cloned.1.call-done) | copy-start | bytes 5971972
  357.8 4.8 copy-start.80
  362.5 5.0 copy-start.60
  362.5 5.0 copy-start.70
  366.6 154.9 %reduce-scatter.6.cloned.1.call-start = ((), (), s32[]{:S(2)}) async-start(), calls=%async_computation.7 | async-start | bytes 2580480 | tf_op jit(solution)/shard_map/reduce_scatter | solution.py:356
  368.5 3.7 copy-start.24
  372.5 3.3 copy-start.26
  372.5 3.3 copy-start.28
  376.5 3.2 copy-start.17
  376.5 3.2 copy-start.32
  379.7 20.1 %copy-start.62 = (f32[128]{0:T(128)S(1)}, f32[128]{0:T(128)}, u32[]{:S(2)}) copy-start(f32[128]{0:T(128)} %copy-done.61) | copy-start | bytes 1540
  379.7 20.1 %copy-start.67 = (f32[128]{0:T(128)S(1)}, f32[128]{0:T(128)}, u32[]{:S(2)}) copy-start(f32[128]{0:T(128)} %copy-done.66) | copy-start | bytes 1540
  381.1 19.7 %copy-start.14 = (bf16[8,128,1152]{2,1,0:T(8,128)(2,1)S(1)}, bf16[8,128,1152]{2,1,0:T(8,128)(2,1)}, u32[]{:S(2)}) copy-start(bf16[8,128,1152]{2,1,0:T(8,128)(2,1)} %exchange_2.1) | copy-start | bytes 7077892
  400.8 5.6 %copy-start.52 = (f32[256]{0:T(256)S(1)}, f32[256]{0:T(256)}, u32[]{:S(2)}) copy-start(f32[256]{0:T(256)} %copy-done.51) | copy-start | bytes 3076
  400.8 5.6 %copy-start.68 = (f32[128]{0:T(128)S(1)}, f32[128]{0:T(128)}, u32[]{:S(2)}) copy-start(f32[128]{0:T(128)} %get-tuple-element.180) | copy-start | bytes 1540
  406.3 3.5 copy-start.9
  406.4 3.5 copy-start.42
  406.4 3.5 copy-start.44
  406.4 3.5 copy-start.74
  409.8 3.9 copy-start.48
  409.9 4.0 copy-start.47
  409.9 4.0 copy-start.46
  433.9 3.4 copy-start.3
  433.9 3.4 copy-start.65
  508.6 4.4 copy-start.56
  510.3 6.0 %copy-start.10 = (bf16[128,1152]{1,0:T(8,128)(2,1)S(1)}, bf16[128,1152]{1,0:T(8,128)(2,1)}, u32[]{:S(2)}) copy-start(bf16[128,1152]{1,0:T(8,128)(2,1)} %refs_2_.1) | copy-start | bytes 884740
  510.3 6.0 %copy-start.30 = (f32[128,1152]{1,0:T(8,128)S(1)}, f32[128,1152]{1,0:T(8,128)}, u32[]{:S(2)}) copy-start(f32[128,1152]{1,0:T(8,128)} %get-tuple-element.197) | copy-start | bytes 1769476
  510.3 6.0 %copy-start.72 = (f32[128]{0:T(128)S(1)}, f32[128]{0:T(128)}, u32[]{:S(2)}) copy-start(f32[128]{0:T(128)} %get-tuple-element.177) | copy-start | bytes 1540
  510.3 6.0 %copy-start.75 = (f32[128]{0:T(128)S(1)}, f32[128]{0:T(128)}, u32[]{:S(2)}) copy-start(f32[128]{0:T(128)} %copy-done.73) | copy-start | bytes 1540
  516.3 7.3 %copy-start.1 = (bf16[256,1152]{1,0:T(8,128)(2,1)S(1)}, bf16[256,1152]{1,0:T(8,128)(2,1)}, u32[]{:S(2)}) copy-start(bf16[256,1152]{1,0:T(8,128)(2,1)} %param.22) | copy-start | bytes 1769476
  (40 other events, 83.0 us)
Sparse Core Ops, SparseCore 0:
  9.6 71.2 all-gather.3
  82.5 44.6 all-gather.5
  128.8 43.9 all-gather.7
  289.7 41.8 reduce-scatter.7
  366.7 43.4 reduce-scatter.3
  412.5 51.4 reduce-scatter.5

commit v2 on v1

--- a/solution.py
+++ b/solution.py
@@ -85,9 +85,14 @@
 
 def swap_kernel(size, axis, kinds, *refs):
     count = len(kinds)
-    ins, outs = refs[:count], refs[count : 2 * count]
-    send, recv, local = refs[2 * count :]
+    ins, outs, kept = refs[:count], refs[count : 2 * count], refs[2 * count : 3 * count]
+    send, recv, local = refs[3 * count :]
     me = lax.axis_index(axis)
+    own = []
+    for item, kind in enumerate(kinds):
+        source = ins[item].at[me] if kind == "swap" else ins[item]
+        own.append(pltpu.make_async_copy(source, kept[item], local.at[item, 0]))
+        own[-1].start()
     barrier = pltpu.get_barrier_semaphore()
     for step in range(1, size):
         peer = lax.rem(me + step, size)
@@ -108,75 +113,90 @@
             )
             copy.start()
             copies.append(copy)
-    for item, kind in enumerate(kinds):
-        source = ins[item].at[me] if kind == "swap" else ins[item]
-        copy = pltpu.make_async_copy(source, outs[item].at[me], local.at[item])
+    for item in range(count):
+        own[item].wait()
+        copy = pltpu.make_async_copy(kept[item], outs[item].at[me], local.at[item, 1])
         copy.start()
         copies.append(copy)
     for copy in copies:
         copy.wait()
 
 
+def chunks_of(rows):
+    for parts in (4, 3, 2):
+        if rows % (16 * parts) == 0:
+            return parts
+    return 1
+
+
 def pair_gather_kernel(size, axis, kinds, *refs):
     count = len(kinds)
-    ins, outs = refs[:count], refs[count : 2 * count]
-    send, recv, pass_send, pass_recv, local = refs[2 * count :]
+    ins, outs, kept = refs[:count], refs[count : 2 * count], refs[2 * count : 3 * count]
+    send, recv, pass_send, pass_recv, local = refs[3 * count :]
     me = lax.axis_index(axis)
     twin = me + 1 - 2 * lax.rem(me, 2)
     half = size // 2
+    own = []
+    for item in range(count):
+        own.append(pltpu.make_async_copy(ins[item], kept[item], local.at[item, 0]))
+        own[-1].start()
     barrier = pltpu.get_barrier_semaphore()
     for step in range(1, half):
         peer = lax.rem(me + 2 * step, size)
         pl.semaphore_signal(barrier, inc=1, device_id={axis: peer}, device_id_type=MESH)
     pl.semaphore_signal(barrier, inc=1, device_id={axis: twin}, device_id_type=MESH)
     pl.semaphore_wait(barrier, half)
-    copies, last = [], []
+    pieces = []
     for item in range(count):
-        row = []
+        rows = ins[item].shape[0]
+        pieces += [
+            (item, part, pl.ds(part * (rows // chunks_of(rows)), rows // chunks_of(rows)))
+            for part in range(chunks_of(rows))
+        ]
+    across, last = [], []
+    for item, part, span in pieces:
         for step in range(1, half):
-            peer = lax.rem(me + 2 * step, size)
             copy = pltpu.make_async_remote_copy(
-                src_ref=ins[item],
-                dst_ref=outs[item].at[me],
-                send_sem=send.at[item, step],
-                recv_sem=recv.at[item, step],
-                device_id={axis: peer},
+                src_ref=ins[item].at[span],
+                dst_ref=outs[item].at[me, span],
+                send_sem=send.at[item, step, part],
+                recv_sem=recv.at[item, step, part],
+                device_id={axis: lax.rem(me + 2 * step, size)},
                 device_id_type=MESH,
             )
             copy.start()
-            row.append(copy)
-        copies.append(row)
-    for item in range(count):
+            across.append((copy, item, step, part, span))
+    for item, part, span in pieces:
         copy = pltpu.make_async_remote_copy(
-            src_ref=ins[item],
-            dst_ref=outs[item].at[me],
-            send_sem=pass_send.at[item, 0],
-            recv_sem=pass_recv.at[item, 0],
+            src_ref=ins[item].at[span],
+            dst_ref=outs[item].at[me, span],
+            send_sem=pass_send.at[item, 0, part],
+            recv_sem=pass_recv.at[item, 0, part],
             device_id={axis: twin},
             device_id_type=MESH,
         )
         copy.start()
         last.append(copy)
-        copy = pltpu.make_async_copy(ins[item], outs[item].at[me], local.at[item])
+    for item in range(count):
+        own[item].wait()
+        copy = pltpu.make_async_copy(kept[item], outs[item].at[me], local.at[item, 1])
         copy.start()
         last.append(copy)
-    for item in range(count):
-        for step in range(1, half):
-            copies[item][step - 1].wait_recv()
-            origin = lax.rem(me + size - 2 * step, size)
-            copy = pltpu.make_async_remote_copy(
-                src_ref=outs[item].at[origin],
-                dst_ref=outs[item].at[origin],
-                send_sem=pass_send.at[item, step],
-                recv_sem=pass_recv.at[item, step],
-                device_id={axis: twin},
-                device_id_type=MESH,
-            )
-            copy.start()
-            last.append(copy)
-    for row in copies:
-        for copy in row:
-            copy.wait_send()
+    for arrived, item, step, part, span in across:
+        arrived.wait_recv()
+        origin = lax.rem(me + size - 2 * step, size)
+        copy = pltpu.make_async_remote_copy(
+            src_ref=outs[item].at[origin, span],
+            dst_ref=outs[item].at[origin, span],
+            send_sem=pass_send.at[item, step, part],
+            recv_sem=pass_recv.at[item, step, part],
+            device_id={axis: twin},
+            device_id_type=MESH,
+        )
+        copy.start()
+        last.append(copy)
+    for sent, *_ in across:
+        sent.wait_send()
     for copy in last:
         copy.wait()
 
@@ -191,10 +211,11 @@
     dma = pltpu.SemaphoreType.DMA
     if pairs:
         half = size // 2
-        scratch = [dma((count, half))] * 4 + [dma((count,))]
+        parts = max(chunks_of(x.shape[0]) for x in arrays)
+        scratch = [dma((count, half, parts))] * 4
         body = pair_gather_kernel
     else:
-        scratch = [dma((count, size - 1))] * 2 + [dma((count,))]
+        scratch = [dma((count, size - 1))] * 2
         body = swap_kernel
     moved = sum(x.size * x.dtype.itemsize for x in shapes)
     return pl.pallas_call(
@@ -202,7 +223,9 @@
         out_shape=shapes,
         in_specs=[pl.BlockSpec(memory_space=pl.ANY)] * count,
         out_specs=tuple(pl.BlockSpec(memory_space=pl.ANY) for _ in arrays),
-        scratch_shapes=scratch,
+        scratch_shapes=[pltpu.VMEM(x.shape[1:], x.dtype) for x in shapes]
+        + scratch
+        + [dma((count, 2))],
         compiler_params=pltpu.CompilerParams(collective_id=ident, has_side_effects=True),
         cost_estimate=pl.CostEstimate(flops=0, bytes_accessed=20 * moved, transcendentals=0),
         name=f"exchange_{ident}",
@@ -248,11 +271,6 @@
     ctx_index = lax.axis_index("ctx")
     query_pos = ctx_index * rows + jnp.arange(rows, dtype=jnp.int32)
     cosine, sine = rope_tables(query_pos.astype(jnp.float32))
-    gate_full, up_full, down_full = (
-        lax.all_gather(gate_weight, "dp", axis=0, tiled=True),
-        lax.all_gather(up_weight, "dp", axis=0, tiled=True),
-        lax.all_gather(down_weight, "dp", axis=0, tiled=True),
-    )
 
     mixed = jnp.concatenate([query_weight, key_weight, value_weight], axis=1)
     mixed_columns = mixed.shape[1] // ctx
@@ -266,6 +284,14 @@
     packed_gains = jnp.concatenate([gain.astype(jnp.float32) for gain in gains])[None]
     mixed_dp, out_dp, gains_dp = exchange(
         (mixed_slice, out_slice, packed_gains), ("gather",) * 3, "dp", dp, 0
+    )
+    gate_weight, up_weight, down_weight, mixed_dp = lax.optimization_barrier(
+        (gate_weight, up_weight, down_weight, mixed_dp)
+    )
+    gate_full, up_full, down_full = (
+        lax.all_gather(gate_weight, "dp", axis=0, tiled=True),
+        lax.all_gather(up_weight, "dp", axis=0, tiled=True),
+        lax.all_gather(down_weight, "dp", axis=0, tiled=True),
     )
     gains_dp = gains_dp[:, 0]
     gain_in, gain_query, gain_key, gain_attn, gain_pre, gain_post = (
@@ -327,6 +353,7 @@
     inv_two = inverse_rms(residual)
     normed_two = (residual * inv_two * gain_pre).astype(bf16)
 
+    attn_all = lax.all_gather(attn_out, "ctx", axis=0, tiled=True)
     (rows_all,) = exchange((normed_two,), ("gather",), "ctx", ctx, 2)
     rows_all = rows_all.reshape(-1, width)
     gate = matmul(rows_all, gate_full)
@@ -343,25 +370,26 @@
     ffn_sum_grad = norm_back(ffn_sum, inv_ffn, gain_post, cot).astype(bf16)
 
     (grad_all,) = exchange((ffn_sum_grad,), ("gather",), "ctx", ctx, 4)
-    grad_all = grad_all.reshape(-1, width)
+    grad_all, attn_all = lax.optimization_barrier((grad_all.reshape(-1, width), attn_all))
     down_shard = lax.psum_scatter(
         matmul_tn(grad_all, hidden).astype(bf16), "dp", scatter_dimension=0, tiled=True
     ).astype(jnp.float32)
     hidden_grad = matmul(grad_all, down_full)
     gate_grad = (hidden_grad * upper * gelu_der).astype(bf16)
     up_grad = (hidden_grad * gelu_val).astype(bf16)
-    gate_shard = lax.psum_scatter(
-        matmul_tn(rows_all, gate_grad).astype(bf16), "dp", scatter_dimension=0, tiled=True
-    ).astype(jnp.float32)
-    up_shard = lax.psum_scatter(
-        matmul_tn(rows_all, up_grad).astype(bf16), "dp", scatter_dimension=0, tiled=True
-    ).astype(jnp.float32)
-    two_part = (matmul_nt(gate_grad, gate_full) + matmul_nt(up_grad, up_full)).astype(bf16)
-    two_parts, attn_all = exchange(
-        (two_part.reshape(ctx, rows, width), attn_out), ("swap", "gather"), "ctx", ctx, 5
-    )
+    two_part, gate_part, up_part = lax.optimization_barrier(
+        (
+            (matmul_nt(gate_grad, gate_full) + matmul_nt(up_grad, up_full)).astype(bf16),
+            matmul_tn(rows_all, gate_grad).astype(bf16),
+            matmul_tn(rows_all, up_grad).astype(bf16),
+        )
+    )
+    gate_shard = lax.psum_scatter(gate_part, "dp", scatter_dimension=0, tiled=True)
+    gate_shard = gate_shard.astype(jnp.float32)
+    up_shard = lax.psum_scatter(up_part, "dp", scatter_dimension=0, tiled=True)
+    up_shard = up_shard.astype(jnp.float32)
+    (two_parts,) = exchange((two_part.reshape(ctx, rows, width),), ("swap",), "ctx", ctx, 5)
     normed_two_grad = sum_blocks(two_parts)
-    attn_all = attn_all.reshape(-1, attn_out.shape[1])
     grad_pre = jnp.sum(normed_two_grad * residual * inv_two, axis=0)
     residual_grad = cot + norm_back(residual, inv_two, gain_pre, normed_two_grad)
     grad_attn = jnp.sum(residual_grad * projected * inv_proj, axis=0)

time: 538 us -> 516 us (0.959)
  Pallas kernels: 329 us -> 281 us
  local copies, waits for them, and re-layouts: 53.7 us -> 74.1 us
  matrix products: 81.8 us -> 89.9 us
    pallas_call x10, Pallas kernels: 329 us -> 281 us  [exchange(): pl.pallas_call(functools.partial(body, size, axis, tuple(kinds)), out_sha...]
    unnamed x172 -> x182, local copies, waits for them, and re-layouts: 9.54 us -> 26.7 us
    dot_general x8, matrix products: 35.4 us -> 44.3 us  [matmul(): return jnp.dot(left, right, preferred_element_type=jnp.float32)]
  transfers between devices with their start and end apart: 6 -> 7, of which waited for: 0 -> 0; matrix products, arithmetic and copies ran while one was open for 31% -> 31% of each run, Pallas kernels for 53% -> 49%
where the time goes in v2:
time: 516 us; the launch traced here: 507 us
  Pallas kernels  281 us (54%)
  matrix products  89.9 us (17%)
  local copies, waits for them, and re-layouts  74.1 us (14%)
  other arithmetic  44.4 us (9%)
  between operations  15.7 us (3%)
    pallas_call x10, Pallas kernels, exchange(): pl.pallas_call(functools.partial(body, size, axis, tuple(kinds)), out_sha...  281 us
    dot_general x8, matrix products, matmul(): return jnp.dot(left, right, preferred_element_type=jnp.float32)  44.3 us
    unnamed x182, local copies, waits for them, and re-layouts  26.7 us
    dot_general x5, matrix products, matmul_nt(): lax.dot_general(left, right, (((1,), (1,)), ((), ())), preferred_element_...  19.1 us
    dot_general x5, matrix products, matmul_tn(): lax.dot_general(left, right, (((0,), (0,)), ((), ())), preferred_element_...  18.2 us
    reduce_sum x8, other arithmetic, sum_blocks(): return jnp.sum(array.astype(jnp.float32), axis=0)  12.3 us
    transpose x2, local copies, waits for them, and re-layouts, from_columns(): return jnp.transpose(array, (1, 0, 2)).reshape(rows, parts * columns)  12 us
  transfers between devices with their start and end apart: 7, of which 0 were waited for; matrix products, arithmetic and copies ran while one was open for 31% of the time, Pallas kernels for 49%

profile of v2, /device:TPU:0, one launch (start us, length us, event | category | flops | bytes accessed | tf_op | source)
XLA Modules:
  0.0 507.2 jit_solution(16465070664063997392)
XLA Ops:
  7.3 4.2 concatenate.29
  12.9 1.8 fusion.72.refs_0_
  14.7 30.8 %exchange_0.1 = (bf16[4,288,192]{2,1,0:T(8,128)(2,1)}, bf16[4,256,144]{2,1,0:T(8,128)(2,1)}, f32[4,1,1280]{2,1,0:T(1,128)}) custom-call(bf16[288,192]{1,0:T(8,128)(2,1)} %fusion.72.refs_0_, bf16[256,144]{1,0:T(8,128)(2,1)} %constant_dynamic-slice_fusion.refs_1_, f32[1,1280]{1,0:T(1,128)} %reshape.399.refs_2_), custom_call_target="tpu_custom_call" | custom-call | bytes 15155200 | tf_op jit(solution)/shard_map/exchange_0/pallas_call | solution.py:221
  48.8 67.2 %exchange_1.1 = (bf16[8,1152,192]{2,1,0:T(8,128)(2,1)}, bf16[8,1024,144]{2,1,0:T(8,128)(2,1)}, bf16[8,128,1152]{2,1,0:T(8,128)(2,1)}) custom-call(bf16[1152,192]{1,0:T(8,128)(2,1)} %bitcast.190, bf16[1024,144]{1,0:T(8,128)(2,1)} %bitcast.193, bf16[128,1152]{1,0:T(8,128)(2,1)} %refs_2_.1), custom_call_target="tpu_custom_call" | custom-call | bytes 165150720 | tf_op jit(solution)/shard_map/exchange_1/pallas_call | solution.py:221
  116.0 2.2 multiply_reduce_fusion
  118.9 6.6 %copy.166 = bf16[1152,8,192]{0,2,1:T(8,128)(2,1)} copy(bf16[1152,8,192]{2,0,1:T(8,128)(2,1)} %bitcast.157) | data formatting | bytes 7077888 | tf_op jit(solution)/shard_map/transpose | solution.py:242
  126.1 2.0 fusion.1
  131.2 2.9 multiply_reduce_fusion.1
  135.6 2.3 fusion.59
  139.2 2.0 fusion.25
  143.1 5.4 %copy.172 = bf16[1024,8,144]{0,2,1:T(8,128)(2,1)S(1)} copy(bf16[1024,8,144]{2,0,1:T(8,128)(2,1)} %bitcast.158) | data formatting | bytes 4718592 | tf_op jit(solution)/shard_map/transpose | solution.py:242
  153.4 18.6 %exchange_2.1 = bf16[8,128,1152]{2,1,0:T(8,128)(2,1)} custom-call(bf16[128,1152]{1,0:T(8,128)(2,1)} %multiply_convert_fusion.4.refs_0_), custom_call_target="tpu_custom_call" | custom-call | bytes 47185920 | tf_op jit(solution)/shard_map/exchange_2/pallas_call | solution.py:221
  173.4 6.6 %fusion.95 = f32[1024,864]{0,1:T(8,128)} fusion(bf16[1024,1152]{1,0:T(8,128)(2,1)} %bitcast.166, bf16[1152,864]{1,0:T(8,128)(2,1)} %all-gather.5.cloned.1.call-done), kind=kOutput, calls=%fused_computation.197 | convolution fusion | flops 2038431744 | bytes 7888896 | tf_op jit(solution)/shard_map/dot_general | solution.py:68
  179.9 9.0 %multiply_convert_fusion.2 = (bf16[1024,864]{0,1:T(8,128)(2,1)}, f32[1024,864]{0,1:T(8,128)}) fusion(f32[1024,864]{0,1:T(8,128)} %fusion.95, bf16[1024,1152]{1,0:T(8,128)(2,1)} %bitcast.167, bf16[1152,864]{1,0:T(8,128)(2,1)} %all-gather.7.cloned.1.call-done), kind=kOutput, calls=%fused_computation.20 | convolution fusion | flops 2047279104 | bytes 13197312 | tf_op jit(solution)/shard_map/dot_general | solution.py:68
  188.9 6.5 %convolution_convert_fusion = bf16[1024,1152]{1,0:T(8,128)(2,1)} fusion(bf16[1024,864]{0,1:T(8,128)(2,1)} %get-tuple-element.222, bf16[1152,864]{1,0:T(8,128)(2,1)} %all-gather.9.cloned.1.call-done), kind=kOutput, calls=%fused_computation.10 | convolution fusion | flops 2039611392 | bytes 6119424 | tf_op jit(solution)/shard_map/dot_general | solution.py:78
  195.4 34.0 %exchange_3.1 = bf16[8,128,1152]{2,1,0:T(8,128)(2,1)} custom-call(bf16[8,128,1152]{2,1,0:T(8,128)(2,1)} %bitcast.171), custom_call_target="tpu_custom_call" | custom-call | bytes 47185920 | tf_op jit(solution)/shard_map/exchange_3/pallas_call | solution.py:221
  229.5 2.1 convert_reduce_fusion.1
  233.6 18.4 %exchange_4.1 = bf16[8,128,1152]{2,1,0:T(8,128)(2,1)} custom-call(bf16[128,1152]{1,0:T(8,128)(2,1)} %get-tuple-element.182.refs_0_), custom_call_target="tpu_custom_call" | custom-call | bytes 47185920 | tf_op jit(solution)/shard_map/exchange_4/pallas_call | solution.py:221
  252.1 19.9 %multiply_convert_fusion.1 = (bf16[1024,864]{0,1:T(8,128)(2,1)S(1)}, bf16[1024,864]{0,1:T(8,128)(2,1)S(1)}) fusion(f32[1024,864]{0,1:T(8,128)} %fusion.95, f32[1024,864]{0,1:T(8,128)} %get-tuple-element.223, bf16[1024,1152]{1,0:T(8,128)(2,1)} %bitcast.164, bf16[1152,864]{1,0:T(8,128)(2,1)} %all-gather.9.cloned.1.call-done), kind=kOutput, calls=%fused_computation.19 | convolution fusion | flops 2058780672 | bytes 14966784 | tf_op jit(solution)/shard_map/dot_general | solution.py:68
  272.0 3.7 convolution_convert_fusion.3
  275.7 3.8 convolution_convert_fusion.2
  279.5 2.9 fusion.96
  282.4 4.4 add_convert_fusion
  286.8 4.1 copy.205
  298.9 2.2 multiply_reduce_fusion.14
  303.7 27.9 %exchange_5.1 = bf16[8,128,1152]{2,1,0:T(8,128)(2,1)} custom-call(bf16[8,128,1152]{2,1,0:T(8,128)(2,1)} %bitcast.170), custom_call_target="tpu_custom_call" | custom-call | bytes 47185920 | tf_op jit(solution)/shard_map/exchange_5/pallas_call | solution.py:221
  331.6 4.1 copy.207
  335.7 2.1 convert_reduce_fusion
  338.6 1.8 multiply_reduce_fusion.3
  343.0 1.9 copy.186
  347.3 2.5 fusion.16
  353.4 2.6 fusion.21
  357.4 15.9 %exchange_6.1 = (bf16[8,128,256]{2,1,0:T(8,128)(2,1)}, bf16[8,128,256]{2,1,0:T(8,128)(2,1)}) custom-call(bf16[8,128,256]{2,1,0:T(8,128)(2,1)} %bitcast.191, bf16[8,128,256]{2,1,0:T(8,128)(2,1)} %bitcast.192), custom_call_target="tpu_custom_call" | custom-call | bytes 20971520 | tf_op jit(solution)/shard_map/exchange_6/pallas_call | solution.py:221
  377.1 5.5 %convolution_convert_fusion.1 = bf16[1152,864]{1,0:T(8,128)(2,1)} fusion(bf16[1024,1152]{1,0:T(8,128)(2,1)S(1)} %bitcast.165, bf16[1024,864]{0,1:T(8,128)(2,1)} %get-tuple-element.222), kind=kOutput, calls=%fused_computation.11 | convolution fusion | flops 2039427072 | bytes 6119424 | tf_op jit(solution)/shard_map/dot_general | solution.py:72
  388.1 3.8 fusion.56
  393.2 17.0 %exchange_7.1 = (bf16[8,128,192]{2,1,0:T(8,128)(2,1)}, bf16[8,128,144]{2,1,0:T(8,128)(2,1)}, f32[8,4,160]{2,1,0:T(4,128)}) custom-call(bf16[8,128,192]{2,1,0:T(8,128)(2,1)} %bitcast.175, bf16[8,128,144]{2,1,0:T(8,128)(2,1)} %bitcast.176, f32[8,4,160]{2,1,0:T(4,128)} %bitcast.195), custom_call_target="tpu_custom_call" | custom-call | bytes 14172160 | tf_op jit(solution)/shard_map/exchange_7/pallas_call | solution.py:221
  410.2 2.7 fusion.9
  412.9 2.1 copy.190
  415.0 2.5 convolution_convert_fusion.5
  419.1 32.3 %exchange_8.1 = (bf16[4,288,192]{2,1,0:T(8,128)(2,1)}, bf16[4,256,144]{2,1,0:T(8,128)(2,1)}, f32[4,1,160]{2,1,0:T(1,128)}) custom-call(bf16[4,288,192]{2,1,0:T(8,128)(2,1)} %bitcast.172, bf16[4,256,144]{2,1,0:T(8,128)(2,1)} %bitcast.177, f32[4,1,160]{2,1,0:T(1,128)} %broadcast_in_dim.33.refs_2_), custom_call_target="tpu_custom_call" | custom-call | bytes 14796800 | tf_op jit(solution)/shard_map/exchange_8/pallas_call | solution.py:221
  451.4 1.9 reduce_sum.317.refs_0_
  453.3 2.1 reduce_sum.318.refs_1_
  456.6 19.0 %exchange_9.1 = (bf16[8,288,192]{2,1,0:T(8,128)(2,1)}, bf16[8,256,144]{2,1,0:T(8,128)(2,1)}, f32[8,1,160]{2,1,0:T(1,128)}) custom-call(bf16[288,192]{1,0:T(8,128)(2,1)} %reduce_sum.317.refs_0_, bf16[256,144]{1,0:T(8,128)(2,1)} %reduce_sum.318.refs_1_, f32[1,160]{1,0:T(1,128)} %bitcast.200), custom_call_target="tpu_custom_call" | custom-call | bytes 29593600 | tf_op jit(solution)/shard_map/exchange_9/pallas_call | solution.py:221
  479.4 2.0 reshape.401
  481.4 2.5 slice.122
  485.7 2.7 copy.194
  489.7 1.9 fusion.90
  497.9 2.1 convert_element_type.223
  (298 shorter events, 69.2 us)
Async XLA Ops:
  7.2 4.9 copy-start
  7.2 41.4 %copy-start.7 = (bf16[128,1152]{1,0:T(8,128)(2,1)S(1)}, bf16[128,1152]{1,0:T(8,128)(2,1)}, u32[]{:S(2)}) copy-start(bf16[128,1152]{1,0:T(8,128)(2,1)} %refs_2_.1) | copy-start | bytes 884740
  7.2 166.2 %all-gather.5.cloned.1.call-start = ((), (), s32[]{:S(2)}) async-start(), calls=%async_computation.3 | async-start | bytes 2580480 | tf_op jit(solution)/shard_map/all_gather | solution.py:292
  45.5 134.4 %all-gather.7.cloned.1.call-start = ((), (), s32[]{:S(2)}) async-start(), calls=%async_computation.4 | async-start | bytes 2580480 | tf_op jit(solution)/shard_map/all_gather | solution.py:293
  46.3 142.6 %all-gather.9.cloned.1.call-start = ((), (), s32[]{:S(2)}) async-start(), calls=%async_computation.5 | async-start | bytes 2580480 | tf_op jit(solution)/shard_map/all_gather | solution.py:294
  47.0 205.0 %all-gather.11.cloned.1.call-start = ((), (), s32[]{:S(2)}) async-start(), calls=%async_computation.6 | async-start | bytes 2359296 | tf_op jit(solution)/shard_map/all_gather | solution.py:356
  48.6 79.5 %copy-start.48 = (f32[1152]{0:T(1024)}, f32[1152]{0:T(1024)S(1)}, u32[]{:S(2)}) copy-start(f32[1152]{0:T(1024)S(1)} %mul.753) | copy-start | bytes 13828
  118.8 7.3 %copy-start.2 = (bf16[8,128,1152]{2,1,0:T(8,128)(2,1)S(1)}, bf16[8,128,1152]{2,1,0:T(8,128)(2,1)}, u32[]{:S(2)}) copy-start(bf16[8,128,1152]{2,1,0:T(8,128)(2,1)} %get-tuple-element.44) | copy-start | bytes 7077892
  125.5 8.8 %copy-start.72 = (f32[128]{0:T(128)}, f32[128]{0:T(128)S(1)}, u32[]{:S(2)}) copy-start(f32[128]{0:T(128)S(1)} %get-tuple-element.228) | copy-start | bytes 1540
  126.1 8.5 %copy-start.60 = (f32[256]{0:T(256)}, f32[256]{0:T(256)S(1)}, u32[]{:S(2)}) copy-start(f32[256]{0:T(256)S(1)} %mul.778) | copy-start | bytes 3076
  130.0 4.7 copy-start.4
  131.2 3.5 copy-start.56
  134.2 3.8 copy-start.57
  134.2 3.8 copy-start.67
  134.3 6.9 %copy-start.37 = (pred[128,1024]{0,1:T(8,128)(4,1)}, pred[128,1024]{0,1:T(8,128)(4,1)S(1)}, u32[]{:S(2)}) copy-start(pred[128,1024]{0,1:T(8,128)(4,1)S(1)} %iota_compare_fusion) | copy-start | bytes 393220
  134.6 3.3 copy-start.31
  135.3 3.2 copy-start.41
  135.3 3.2 copy-start.42
  143.0 349.7 %reduce-scatter.10.cloned.1.call-start = ((), (), s32[]{:S(2)}) async-start(), calls=%async_computation.8 | async-start | bytes 2580480
  143.1 5.4 %copy-start.16 = (bf16[128,4,256]{0,2,1:T(8,128)(2,1)S(1)}, bf16[128,4,256]{0,2,1:T(8,128)(2,1)}, u32[]{:S(2)}) copy-start(bf16[128,4,256]{0,2,1:T(8,128)(2,1)} %copy.171) | copy-start | bytes 786436
  252.1 19.9 %copy-start.14 = (bf16[8,128,1152]{2,1,0:T(8,128)(2,1)S(1)}, bf16[8,128,1152]{2,1,0:T(8,128)(2,1)}, u32[]{:S(2)}) copy-start(bf16[8,128,1152]{2,1,0:T(8,128)(2,1)} %exchange_2.1) | copy-start | bytes 7077892
  275.7 3.8 copy-start.80
  290.9 204.3 %reduce-scatter.12.cloned.1.call-start = ((), (), s32[]{:S(2)}) async-start(), calls=%async_computation.9 | async-start | bytes 2580480
  295.8 6.0 %copy-start.63 = (f32[4,128]{1,0:T(4,128)S(1)}, f32[4,128]{1,0:T(4,128)}, u32[]{:S(2)}) copy-start(f32[4,128]{1,0:T(4,128)} %copy-done.62) | copy-start | bytes 6148
  295.8 6.0 %copy-start.65 = (f32[4,128]{1,0:T(4,128)S(1)}, f32[4,128]{1,0:T(4,128)}, u32[]{:S(2)}) copy-start(f32[4,128]{1,0:T(4,128)} %copy-done.64) | copy-start | bytes 6148
  340.4 157.5 %reduce-scatter.8.cloned.1.call-start = ((), (), s32[]{:S(2)}) async-start(), calls=%async_computation.7 | async-start | bytes 2580480 | tf_op jit(solution)/shard_map/reduce_scatter | solution.py:374
  343.0 3.7 copy-start.26
  347.2 3.1 copy-start.32
  347.3 3.1 copy-start.34
  351.3 4.7 copy-start.18
  351.4 4.7 copy-start.28
  352.3 3.7 copy-start.38
  356.0 20.1 %copy-start.68 = (f32[128]{0:T(128)S(1)}, f32[128]{0:T(128)}, u32[]{:S(2)}) copy-start(f32[128]{0:T(128)} %copy-done.67) | copy-start | bytes 1540
  356.0 20.1 %copy-start.73 = (f32[128]{0:T(128)S(1)}, f32[128]{0:T(128)}, u32[]{:S(2)}) copy-start(f32[128]{0:T(128)} %copy-done.72) | copy-start | bytes 1540
  357.4 19.7 %copy-start.13 = (bf16[8,128,1152]{2,1,0:T(8,128)(2,1)S(1)}, bf16[8,128,1152]{2,1,0:T(8,128)(2,1)}, u32[]{:S(2)}) copy-start(bf16[8,128,1152]{2,1,0:T(8,128)(2,1)} %exchange_4.1) | copy-start | bytes 7077892
  377.1 5.5 %copy-start.58 = (f32[256]{0:T(256)S(1)}, f32[256]{0:T(256)}, u32[]{:S(2)}) copy-start(f32[256]{0:T(256)} %copy-done.57) | copy-start | bytes 3076
  377.1 5.6 %copy-start.74 = (f32[128]{0:T(128)S(1)}, f32[128]{0:T(128)}, u32[]{:S(2)}) copy-start(f32[128]{0:T(128)} %get-tuple-element.209) | copy-start | bytes 1540
  382.7 3.1 copy-start.47
  388.1 4.1 copy-start.52
  388.1 4.2 copy-start.51
  388.1 4.2 copy-start.54
  388.1 22.1 %copy-start.3 = (bf16[8,128,1152]{2,1,0:T(8,128)(2,1)S(1)}, bf16[8,128,1152]{2,1,0:T(8,128)(2,1)}, u32[]{:S(2)}) copy-start(bf16[8,128,1152]{2,1,0:T(8,128)(2,1)} %get-tuple-element.44) | copy-start | bytes 7077892
  388.1 22.1 %copy-start.71 = (f32[8,128]{1,0:T(8,128)S(1)}, f32[8,128]{1,0:T(8,128)}, u32[]{:S(2)}) copy-start(f32[8,128]{1,0:T(8,128)} %get-tuple-element.200) | copy-start | bytes 12292
  412.9 5.6 %copy-start.53 = (f32[8,4,160]{2,1,0:T(4,128)S(1)}, f32[8,4,160]{2,1,0:T(4,128)}, u32[]{:S(2)}) copy-start(f32[8,4,160]{2,1,0:T(4,128)} %get-tuple-element.58) | copy-start | bytes 61444
  485.7 5.9 %copy-start.36 = (f32[128,1152]{1,0:T(8,128)S(1)}, f32[128,1152]{1,0:T(8,128)}, u32[]{:S(2)}) copy-start(f32[128,1152]{1,0:T(8,128)} %get-tuple-element.226) | copy-start | bytes 1769476
  485.7 5.9 %copy-start.77 = (f32[128]{0:T(128)S(1)}, f32[128]{0:T(128)}, u32[]{:S(2)}) copy-start(f32[128]{0:T(128)} %get-tuple-element.206) | copy-start | bytes 1540
  485.7 5.9 %copy-start.79 = (f32[128]{0:T(128)S(1)}, f32[128]{0:T(128)}, u32[]{:S(2)}) copy-start(f32[128]{0:T(128)} %copy-done.78) | copy-start | bytes 1540
  494.0 5.9 %copy-start.1 = (bf16[256,1152]{1,0:T(8,128)(2,1)S(1)}, bf16[256,1152]{1,0:T(8,128)(2,1)}, u32[]{:S(2)}) copy-start(bf16[256,1152]{1,0:T(8,128)(2,1)} %param.22) | copy-start | bytes 1769476
  (43 other events, 81.0 us)
Sparse Core Ops, SparseCore 0:
  45.7 45.1 all-gather.4
  92.5 43.9 all-gather.6
  138.0 43.9 all-gather.8
  184.3 41.1 all-gather.10
  291.1 41.8 reduce-scatter.9
  340.5 43.0 reduce-scatter.11
  385.9 47.1 reduce-scatter.7

commit v3 on v2

--- a/solution.py
+++ b/solution.py
@@ -272,21 +272,27 @@
     query_pos = ctx_index * rows + jnp.arange(rows, dtype=jnp.int32)
     cosine, sine = rope_tables(query_pos.astype(jnp.float32))
 
-    mixed = jnp.concatenate([query_weight, key_weight, value_weight], axis=1)
-    mixed_columns = mixed.shape[1] // ctx
+    qwidth = query_weight.shape[1]
+    kwidth = key_weight.shape[1]
+    mixed_columns = (qwidth + 2 * kwidth) // ctx
     out_columns = out_weight.shape[1] // ctx
-    mixed_slice = lax.dynamic_slice_in_dim(mixed, ctx_index * mixed_columns, mixed_columns, 1)
-    out_slice = lax.dynamic_slice_in_dim(out_weight, ctx_index * out_columns, out_columns, 1)
+    query_columns = qwidth // ctx
+    pair = jnp.concatenate([key_weight, value_weight], axis=1)
+    pair_rows = pair.shape[0] // ctx
+    out_rows = out_weight.shape[0] // ctx
+    query_slice = lax.dynamic_slice_in_dim(query_weight, ctx_index * query_columns, query_columns, 1)
+    pair_slice = lax.dynamic_slice_in_dim(pair, ctx_index * pair_rows, pair_rows, 0)
+    out_slice = lax.dynamic_slice_in_dim(out_weight, ctx_index * out_rows, out_rows, 0)
     gains = (in_gain, query_gain, key_gain, attn_post_gain, ffn_pre_gain, ffn_post_gain)
     cuts = [0]
     for gain in gains:
         cuts.append(cuts[-1] + gain.shape[0])
     packed_gains = jnp.concatenate([gain.astype(jnp.float32) for gain in gains])[None]
-    mixed_dp, out_dp, gains_dp = exchange(
-        (mixed_slice, out_slice, packed_gains), ("gather",) * 3, "dp", dp, 0
-    )
-    gate_weight, up_weight, down_weight, mixed_dp = lax.optimization_barrier(
-        (gate_weight, up_weight, down_weight, mixed_dp)
+    query_dp, pair_dp, out_dp, gains_dp = exchange(
+        (query_slice, pair_slice, out_slice, packed_gains), ("gather",) * 4, "dp", dp, 0
+    )
+    gate_weight, up_weight, down_weight, query_dp = lax.optimization_barrier(
+        (gate_weight, up_weight, down_weight, query_dp)
     )
     gate_full, up_full, down_full = (
         lax.all_gather(gate_weight, "dp", axis=0, tiled=True),
@@ -297,24 +303,18 @@
     gain_in, gain_query, gain_key, gain_attn, gain_pre, gain_post = (
         gains_dp[:, low:high].reshape(-1) for low, high in zip(cuts[:-1], cuts[1:])
     )
-    mixed_all, out_all, tokens_all = exchange(
-        (
-            mixed_dp.reshape(-1, mixed_columns),
-            out_dp.reshape(-1, out_columns),
-            tokens,
-        ),
-        ("gather",) * 3,
+    query_all, pair_all, out_all, tokens_all = exchange(
+        (query_dp.reshape(-1, query_columns), pair_dp, out_dp, tokens),
+        ("gather",) * 4,
         "ctx",
         ctx,
         1,
     )
-    mixed_full = from_columns(mixed_all)
-    out_full = from_columns(out_all)
-    qwidth = query_weight.shape[1]
-    kwidth = key_weight.shape[1]
-    query_full = mixed_full[:, :qwidth]
-    key_full = mixed_full[:, qwidth : qwidth + kwidth]
-    value_full = mixed_full[:, qwidth + kwidth :]
+    query_full = from_columns(query_all)
+    pair_full = jnp.transpose(pair_all, (1, 0, 2, 3)).reshape(-1, 2 * kwidth)
+    key_full = pair_full[:, :kwidth]
+    value_full = pair_full[:, kwidth:]
+    out_full = jnp.transpose(out_all, (1, 0, 2, 3)).reshape(-1, out_weight.shape[1])
 
     inputs_f = tokens.astype(jnp.float32)
     inv_one = inverse_rms(inputs_f)
@@ -371,9 +371,11 @@
 
     (grad_all,) = exchange((ffn_sum_grad,), ("gather",), "ctx", ctx, 4)
     grad_all, attn_all = lax.optimization_barrier((grad_all.reshape(-1, width), attn_all))
-    down_shard = lax.psum_scatter(
-        matmul_tn(grad_all, hidden).astype(bf16), "dp", scatter_dimension=0, tiled=True
-    ).astype(jnp.float32)
+    down_part, grad_all = lax.optimization_barrier(
+        (matmul_tn(grad_all, hidden).astype(bf16), grad_all)
+    )
+    down_shard = lax.psum_scatter(down_part, "dp", scatter_dimension=0, tiled=True)
+    down_shard = down_shard.astype(jnp.float32)
     hidden_grad = matmul(grad_all, down_full)
     gate_grad = (hidden_grad * upper * gelu_der).astype(bf16)
     up_grad = (hidden_grad * gelu_val).astype(bf16)
@@ -432,21 +434,24 @@
     grad_kgain = jnp.sum(key_normed_grad * keys * inv_key, axis=0)
     key_grad = norm_back(keys, inv_key, gain_key, key_normed_grad).astype(bf16)
     mixed_grad = jnp.concatenate([query_grad, key_grad, value_grad], axis=1)
-    normed_one_grad = matmul_nt(mixed_grad, mixed_full)
+    normed_one_grad = matmul_nt(query_grad, query_full) + matmul_nt(
+        mixed_grad[:, qwidth:], pair_full
+    )
     grad_in = jnp.sum(normed_one_grad * inputs_f * inv_one, axis=0)
     input_grad = residual_grad + norm_back(inputs_f, inv_one, gain_in, normed_one_grad)
 
     gain_grads = (grad_in, grad_qgain, grad_kgain, grad_attn, grad_pre, grad_post)
     packed = jnp.concatenate([grad.reshape(dp, -1) for grad in gain_grads], axis=1)
-    mixed_cols, out_cols, gain_parts = exchange(
-        (by_columns(mixed_grad, ctx), by_columns(projected_grad, ctx), by_columns(packed, ctx)),
-        ("swap",) * 3,
+    both = jnp.concatenate([by_columns(mixed_grad, ctx), by_columns(projected_grad, ctx)], axis=2)
+    both, gain_parts = exchange(
+        (both, by_columns(packed, ctx)),
+        ("swap",) * 2,
         "ctx",
         ctx,
         7,
     )
-    mixed_w = matmul_tn(normed_all, mixed_cols.reshape(-1, mixed_columns)).astype(bf16)
-    out_w = matmul_tn(attn_all, out_cols.reshape(-1, out_columns)).astype(bf16)
+    mixed_w = matmul_tn(normed_all, both[:, :, :mixed_columns].reshape(-1, mixed_columns)).astype(bf16)
+    out_w = matmul_tn(attn_all, both[:, :, mixed_columns:].reshape(-1, out_columns)).astype(bf16)
     mixed_w, out_w, gain_parts = exchange(
         (
             mixed_w.reshape(dp, -1, mixed_columns),

time: 516 us -> 490 us (0.950)
  Pallas kernels: 281 us -> 258 us
  matrix products: 89.9 us -> 71.7 us
  waiting for transfers between devices: 1.49 us -> 13 us
  other arithmetic: 44.4 us -> 49.8 us
    pallas_call x10, Pallas kernels: 281 us -> 258 us  [exchange(): pl.pallas_call(functools.partial(body, size, axis, tuple(kinds)), out_sha...]
    dot_general x8, matrix products: 44.3 us -> 28.3 us  [matmul(): return jnp.dot(left, right, preferred_element_type=jnp.float32)]
    all_gather x1, waiting for transfers between devices: 0.01 us -> 11.5 us  [on_device(): lax.all_gather(down_weight, 'dp', axis=0, tiled=True)]
    transpose x2 -> x1, local copies, waits for them, and re-layouts: 12 us -> 3.02 us  [from_columns(): return jnp.transpose(array, (1, 0, 2)).reshape(rows, parts * columns)]
    unnamed x182 -> x165, local copies, waits for them, and re-layouts: 26.7 us -> 32.1 us
    dot_general x5 -> x6, matrix products: 19.1 us -> 15.7 us  [matmul_nt(): lax.dot_general(left, right, (((1,), (1,)), ((), ())), preferred_element_...]
  transfers between devices with their start and end apart: 7 -> 7, of which waited for: 0 -> 1; matrix products, arithmetic and copies ran while one was open for 31% -> 30% of each run, Pallas kernels for 49% -> 49%
where the time goes in v3:
time: 490 us; the launch traced here: 481 us
  Pallas kernels  258 us (53%)
  local copies, waits for them, and re-layouts  72.7 us (15%)
  matrix products  71.7 us (15%)
  other arithmetic  49.8 us (10%)
  between operations  15.4 us (3%)
  waiting for transfers between devices  13 us (3%)
    pallas_call x10, Pallas kernels, exchange(): pl.pallas_call(functools.partial(body, size, axis, tuple(kinds)), out_sha...  258 us
    unnamed x165, local copies, waits for them, and re-layouts  32.1 us
    dot_general x8, matrix products, matmul(): return jnp.dot(left, right, preferred_element_type=jnp.float32)  28.3 us
    dot_general x5, matrix products, matmul_tn(): lax.dot_general(left, right, (((0,), (0,)), ((), ())), preferred_element_...  19.3 us
    dot_general x6, matrix products, matmul_nt(): lax.dot_general(left, right, (((1,), (1,)), ((), ())), preferred_element_...  15.7 us
    all_gather x1, waiting for transfers between devices, on_device(): lax.all_gather(down_weight, 'dp', axis=0, tiled=True)  11.5 us
    reduce_sum x8, other arithmetic, sum_blocks(): return jnp.sum(array.astype(jnp.float32), axis=0)  11.4 us
  transfers between devices with their start and end apart: 7, of which 1 were waited for; matrix products, arithmetic and copies ran while one was open for 30% of the time, Pallas kernels for 49%

profile of v3, /device:TPU:0, one launch (start us, length us, event | category | flops | bytes accessed | tf_op | source)
XLA Modules:
  0.0 481.5 jit_solution(9725981886471831568)
XLA Ops:
  7.3 4.2 concatenate.33
  15.7 23.1 %exchange_0.1 = (bf16[4,288,128]{2,1,0:T(8,128)(2,1)}, bf16[4,36,512]{2,1,0:T(8,128)(2,1)}, bf16[4,32,1152]{2,1,0:T(8,128)(2,1)}, f32[4,1,1280]{2,1,0:T(1,128)}) custom-call(bf16[288,128]{1,0:T(8,128)(2,1)} %constant_dynamic-slice_fusion.1.refs_0_, bf16[36,512]{1,0:T(8,128)(2,1)} %fusion.74.refs_1_, bf16[32,1152]{1,0:T(8,128)(2,1)} %constant_dynamic-slice_fusion.refs_2_, ...), custom_call_target="tpu_custom_call" | custom-call | bytes 15155200 | tf_op jit(solution)/shard_map/exchange_0/pallas_call | solution.py:221
  41.5 52.4 %exchange_1.1 = (bf16[8,1152,128]{2,1,0:T(8,128)(2,1)}, bf16[8,4,36,512]{3,2,1,0:T(8,128)(2,1)}, bf16[8,4,32,1152]{3,2,1,0:T(8,128)(2,1)}, bf16[8,128,1152]{2,1,0:T(8,128)(2,1)}) custom-call(bf16[1152,128]{1,0:T(8,128)(2,1)} %bitcast.177, bf16[4,36,512]{2,1,0:T(8,128)(2,1)} %get-tuple-element.46.refs_1_, bf16[4,32,1152]{2,1,0:T(8,128)(2,1)} %get-tuple-element.47.refs_2_, ...), custom_call_target="tpu_custom_call" | custom-call | bytes 165150720 | tf_op jit(solution)/shard_map/exchange_1/pallas_call | solution.py:221
  93.9 2.3 multiply_reduce_fusion
  98.1 3.0 copy.69
  101.7 3.8 fusion.1
  107.2 2.7 multiply_reduce_fusion.1
  111.2 2.3 fusion.57
  120.7 1.9 copy.73
  128.7 18.8 %exchange_2.1 = bf16[8,128,1152]{2,1,0:T(8,128)(2,1)} custom-call(bf16[128,1152]{1,0:T(8,128)(2,1)} %multiply_convert_fusion.4.refs_0_), custom_call_target="tpu_custom_call" | custom-call | bytes 47185920 | tf_op jit(solution)/shard_map/exchange_2/pallas_call | solution.py:221
  148.2 6.6 %fusion.95 = f32[1024,864]{0,1:T(8,128)} fusion(bf16[1024,1152]{1,0:T(8,128)(2,1)} %bitcast.153, bf16[1152,864]{1,0:T(8,128)(2,1)} %all-gather.5.cloned.1.call-done), kind=kOutput, calls=%fused_computation.198 | convolution fusion | flops 2038431744 | bytes 7888896 | tf_op jit(solution)/shard_map/dot_general | solution.py:68
  154.8 9.0 %multiply_convert_fusion.2 = (bf16[1024,864]{0,1:T(8,128)(2,1)}, f32[1024,864]{0,1:T(8,128)}) fusion(f32[1024,864]{0,1:T(8,128)} %fusion.95, bf16[1024,1152]{1,0:T(8,128)(2,1)} %bitcast.154, bf16[1152,864]{1,0:T(8,128)(2,1)} %all-gather.7.cloned.1.call-done), kind=kOutput, calls=%fused_computation.19 | convolution fusion | flops 2047279104 | bytes 13197312 | tf_op jit(solution)/shard_map/dot_general | solution.py:68
  163.8 11.5 %all-gather.9.cloned.1.call-done = bf16[1152,864]{1,0:T(8,128)(2,1)} async-done(((bf16[288,864]{1,0:T(8,128)(2,1)}), bf16[1152,864]{1,0:T(8,128)(2,1)}) %all-gather.9.cloned.1.call-update) | async-done | bytes 1990672 | tf_op jit(solution)/shard_map/all_gather | solution.py:300
  175.3 6.4 %convolution_convert_fusion = bf16[1024,1152]{1,0:T(8,128)(2,1)} fusion(bf16[1024,864]{0,1:T(8,128)(2,1)} %get-tuple-element.183, bf16[1152,864]{1,0:T(8,128)(2,1)} %all-gather.9.cloned.1.call-done), kind=kOutput, calls=%fused_computation.10 | convolution fusion | flops 2039611392 | bytes 6119424 | tf_op jit(solution)/shard_map/dot_general | solution.py:78
  181.7 36.3 %exchange_3.1 = bf16[8,128,1152]{2,1,0:T(8,128)(2,1)} custom-call(bf16[8,128,1152]{2,1,0:T(8,128)(2,1)} %bitcast.161), custom_call_target="tpu_custom_call" | custom-call | bytes 47185920 | tf_op jit(solution)/shard_map/exchange_3/pallas_call | solution.py:221
  218.1 2.1 convert_reduce_fusion.1
  222.2 19.1 %exchange_4.1 = bf16[8,128,1152]{2,1,0:T(8,128)(2,1)} custom-call(bf16[128,1152]{1,0:T(8,128)(2,1)} %get-tuple-element.143.refs_0_), custom_call_target="tpu_custom_call" | custom-call | bytes 47185920 | tf_op jit(solution)/shard_map/exchange_4/pallas_call | solution.py:221
  241.4 6.5 %convolution_convert_fusion.3 = bf16[1152,864]{0,1:T(8,128)(2,1)} fusion(bf16[1024,864]{0,1:T(8,128)(2,1)} %get-tuple-element.183, bf16[1024,1152]{1,0:T(8,128)(2,1)} %bitcast.159), kind=kOutput, calls=%fused_computation.22 | convolution fusion | flops 2039427072 | bytes 6119424 | tf_op jit(solution)/shard_map/dot_general | solution.py:72
  247.9 4.8 %multiply_convert_fusion.1 = (bf16[1024,864]{0,1:T(8,128)(2,1)S(1)}, bf16[1024,864]{0,1:T(8,128)(2,1)S(1)}) fusion(f32[1024,864]{0,1:T(8,128)S(1)} %copy-done.75, f32[1024,864]{0,1:T(8,128)S(1)} %copy-done.76, bf16[1024,1152]{1,0:T(8,128)(2,1)S(1)} %bitcast.160, bf16[1152,864]{1,0:T(8,128)(2,1)S(1)} %copy-done.72), kind=kOutput, calls=%fused_computation.18 | convolution fusion | flops 2058780672 | bytes 14966784 | tf_op jit(solution)/shard_map/dot_general | solution.py:68
  252.7 3.8 convolution_convert_fusion.2
  256.5 3.7 convolution_convert_fusion.1
  260.3 2.9 fusion.96
  263.2 4.3 add_convert_fusion
  267.5 4.1 copy.104
  271.9 2.0 multiply_reduce_fusion.15
  277.2 27.7 %exchange_5.1 = bf16[8,128,1152]{2,1,0:T(8,128)(2,1)} custom-call(bf16[8,128,1152]{2,1,0:T(8,128)(2,1)} %bitcast.157), custom_call_target="tpu_custom_call" | custom-call | bytes 47185920 | tf_op jit(solution)/shard_map/exchange_5/pallas_call | solution.py:221
  304.9 4.1 copy.106
  309.0 2.1 convert_reduce_fusion
  313.6 2.3 multiply_reduce_fusion.3
  319.9 4.1 copy.108
  325.1 2.6 fusion.14
  330.4 16.1 %exchange_6.1 = (bf16[8,128,256]{2,1,0:T(8,128)(2,1)}, bf16[8,128,256]{2,1,0:T(8,128)(2,1)}) custom-call(bf16[8,128,256]{2,1,0:T(8,128)(2,1)} %bitcast.175, bf16[8,128,256]{2,1,0:T(8,128)(2,1)} %bitcast.176), custom_call_target="tpu_custom_call" | custom-call | bytes 20971520 | tf_op jit(solution)/shard_map/exchange_6/pallas_call | solution.py:221
  347.7 2.0 fusion.21
  355.2 2.0 copy.85
  365.3 2.4 pad_maximum_fusion.refs_0_
  367.7 13.9 %exchange_7.1 = (bf16[8,128,336]{2,1,0:T(8,128)(2,1)}, f32[8,4,160]{2,1,0:T(4,128)}) custom-call(bf16[8,128,336]{2,1,0:T(8,128)(2,1)} %pad_maximum_fusion.refs_0_, f32[8,4,160]{2,1,0:T(4,128)} %bitcast.178), custom_call_target="tpu_custom_call" | custom-call | bytes 14172160 | tf_op jit(solution)/shard_map/exchange_7/pallas_call | solution.py:221
  381.6 2.1 slice.100
  383.7 2.7 fusion.9
  386.4 2.1 copy.88
  388.5 2.5 convolution_convert_fusion.5
  392.7 31.7 %exchange_8.1 = (bf16[4,288,192]{2,1,0:T(8,128)(2,1)}, bf16[4,256,144]{2,1,0:T(8,128)(2,1)}, f32[4,1,160]{2,1,0:T(1,128)}) custom-call(bf16[4,288,192]{2,1,0:T(8,128)(2,1)} %bitcast.162, bf16[4,256,144]{2,1,0:T(8,128)(2,1)} %bitcast.167, f32[4,1,160]{2,1,0:T(1,128)} %broadcast_in_dim.33.refs_2_), custom_call_target="tpu_custom_call" | custom-call | bytes 14796800 | tf_op jit(solution)/shard_map/exchange_8/pallas_call | solution.py:221
  424.4 1.9 reduce_sum.308.refs_0_
  426.3 1.8 reduce_sum.309.refs_1_
  429.4 19.0 %exchange_9.1 = (bf16[8,288,192]{2,1,0:T(8,128)(2,1)}, bf16[8,256,144]{2,1,0:T(8,128)(2,1)}, f32[8,1,160]{2,1,0:T(1,128)}) custom-call(bf16[288,192]{1,0:T(8,128)(2,1)} %reduce_sum.308.refs_0_, bf16[256,144]{1,0:T(8,128)(2,1)} %reduce_sum.309.refs_1_, f32[1,160]{1,0:T(1,128)} %bitcast.182), custom_call_target="tpu_custom_call" | custom-call | bytes 29593600 | tf_op jit(solution)/shard_map/exchange_9/pallas_call | solution.py:221
  450.6 2.8 copy.90
  453.4 2.3 reshape.393
  459.6 2.7 copy.92
  463.6 1.9 fusion.90
  (277 shorter events, 75.6 us)
Async XLA Ops:
  7.2 4.9 %copy-start = (bf16[288,1024]{1,0:T(8,128)(2,1)S(1)}, bf16[288,1024]{1,0:T(8,128)(2,1)}, u32[]{:S(2)}) copy-start(bf16[288,1024]{1,0:T(8,128)(2,1)} %param.17) | copy-start | bytes 1769476
  7.2 34.1 %copy-start.4 = (bf16[128,1152]{1,0:T(8,128)(2,1)S(1)}, bf16[128,1152]{1,0:T(8,128)(2,1)}, u32[]{:S(2)}) copy-start(bf16[128,1152]{1,0:T(8,128)(2,1)} %refs_3_.1) | copy-start | bytes 884740
  7.2 141.0 %all-gather.5.cloned.1.call-start = ((), (), s32[]{:S(2)}) async-start(), calls=%async_computation.3 | async-start | bytes 2580480 | tf_op jit(solution)/shard_map/all_gather | solution.py:298
  38.8 116.0 %all-gather.7.cloned.1.call-start = ((), (), s32[]{:S(2)}) async-start(), calls=%async_computation.4 | async-start | bytes 2580480 | tf_op jit(solution)/shard_map/all_gather | solution.py:299
  39.5 135.8 %all-gather.9.cloned.1.call-start = ((), (), s32[]{:S(2)}) async-start(), calls=%async_computation.5 | async-start | bytes 2580480 | tf_op jit(solution)/shard_map/all_gather | solution.py:300
  40.3 201.0 %all-gather.11.cloned.1.call-start = ((), (), s32[]{:S(2)}) async-start(), calls=%async_computation.6 | async-start | bytes 2359296 | tf_op jit(solution)/shard_map/all_gather | solution.py:356
  40.3 69.7 %copy-start.65 = (f32[128]{0:T(128)}, f32[128]{0:T(128)S(1)}, u32[]{:S(2)}) copy-start(f32[128]{0:T(128)S(1)} %get-tuple-element.189) | copy-start | bytes 1540
  101.7 3.9 copy-start.61
  101.7 8.7 %copy-start.50 = (f32[256]{0:T(256)}, f32[256]{0:T(256)S(1)}, u32[]{:S(2)}) copy-start(f32[256]{0:T(256)S(1)} %mul.759) | copy-start | bytes 3076
  101.7 3.8 copy-start.5
  106.5 4.1 copy-start.7
  107.1 3.4 copy-start.42
  107.2 3.8 copy-start.48
  109.9 3.6 copy-start.57
  110.0 7.8 %copy-start.31 = (pred[128,1024]{0,1:T(8,128)(4,1)}, pred[128,1024]{0,1:T(8,128)(4,1)S(1)}, u32[]{:S(2)}) copy-start(pred[128,1024]{0,1:T(8,128)(4,1)S(1)} %iota_compare_fusion) | copy-start | bytes 393220
  111.0 3.7 copy-start.35
  111.0 3.7 copy-start.37
  120.4 346.2 %reduce-scatter.10.cloned.1.call-start = ((), (), s32[]{:S(2)}) async-start(), calls=%async_computation.7 | async-start | bytes 2580480
  120.7 3.3 copy-start.19
  125.9 21.6 %copy-start.55 = (f32[128]{0:T(128)}, f32[128]{0:T(128)S(1)}, u32[]{:S(2)}) copy-start(f32[128]{0:T(128)S(1)} %get-tuple-element.170) | copy-start | bytes 1540
  126.0 21.5 %copy-start.39 = (f32[1152]{0:T(1024)}, f32[1152]{0:T(1024)S(1)}, u32[]{:S(2)}) copy-start(f32[1152]{0:T(1024)S(1)} %mul.781) | copy-start | bytes 13828
  127.8 26.9 %copy-start.59 = (f32[128]{0:T(128)}, f32[128]{0:T(128)S(1)}, u32[]{:S(2)}) copy-start(f32[128]{0:T(128)S(1)} %get-tuple-element.172) | copy-start | bytes 1540
  241.3 6.6 %copy-start.17 = (bf16[8,128,1152]{2,1,0:T(8,128)(2,1)S(1)}, bf16[8,128,1152]{2,1,0:T(8,128)(2,1)}, u32[]{:S(2)}) copy-start(bf16[8,128,1152]{2,1,0:T(8,128)(2,1)} %exchange_4.1) | copy-start | bytes 7077892
  241.3 6.5 %copy-start.72 = (bf16[1152,864]{1,0:T(8,128)(2,1)S(1)}, bf16[1152,864]{1,0:T(8,128)(2,1)}, u32[]{:S(2)}) copy-start(bf16[1152,864]{1,0:T(8,128)(2,1)} %all-gather.9.cloned.1.call-done) | copy-start | bytes 5971972
  241.3 6.5 %copy-start.75 = (f32[1024,864]{0,1:T(8,128)S(1)}, f32[1024,864]{0,1:T(8,128)}, u32[]{:S(2)}) copy-start(f32[1024,864]{0,1:T(8,128)} %fusion.95) | copy-start | bytes 10616836
  241.3 6.5 %copy-start.76 = (f32[1024,864]{0,1:T(8,128)S(1)}, f32[1024,864]{0,1:T(8,128)}, u32[]{:S(2)}) copy-start(f32[1024,864]{0,1:T(8,128)} %get-tuple-element.184) | copy-start | bytes 10616836
  247.9 4.8 %copy-start.16 = (bf16[8,128,1152]{2,1,0:T(8,128)(2,1)S(1)}, bf16[8,128,1152]{2,1,0:T(8,128)(2,1)}, u32[]{:S(2)}) copy-start(bf16[8,128,1152]{2,1,0:T(8,128)(2,1)} %exchange_2.1) | copy-start | bytes 7077892
  256.5 3.7 copy-start.70
  271.7 197.5 %reduce-scatter.12.cloned.1.call-start = ((), (), s32[]{:S(2)}) async-start(), calls=%async_computation.8 | async-start | bytes 2580480
  312.7 159.1 %reduce-scatter.14.cloned.1.call-start = ((), (), s32[]{:S(2)}) async-start(), calls=%async_computation.9 | async-start | bytes 2580480
  312.7 3.9 copy-start.56
  312.8 3.9 copy-start.68
  312.8 5.2 %copy-start.3 = (bf16[4,8,32,1152]{3,2,1,0:T(8,128)(2,1)S(1)}, bf16[4,8,32,1152]{3,2,1,0:T(8,128)(2,1)}, u32[]{:S(2)}) copy-start(bf16[4,8,32,1152]{3,2,1,0:T(8,128)(2,1)} %copy-done.2) | copy-start | bytes 7077892
  319.0 5.0 %copy-start.25 = (bf16[128,4,256]{2,0,1:T(8,128)(2,1)S(1)}, bf16[128,4,256]{2,0,1:T(8,128)(2,1)}, u32[]{:S(2)}) copy-start(bf16[128,4,256]{2,0,1:T(8,128)(2,1)} %copy-done.24) | copy-start | bytes 786436
  319.9 5.2 %copy-start.67 = (f32[4,128]{1,0:T(4,128)S(1)}, f32[4,128]{1,0:T(4,128)}, u32[]{:S(2)}) copy-start(f32[4,128]{1,0:T(4,128)} %log_add_fusion) | copy-start | bytes 6148
  325.1 3.9 copy-start.21
  325.1 3.9 copy-start.32
  330.4 19.3 %copy-start.28 = (f32[128,128]{1,0:T(8,128)S(1)}, f32[128,128]{1,0:T(8,128)}, u32[]{:S(2)}) copy-start(f32[128,128]{1,0:T(8,128)} %copy-done.27) | copy-start | bytes 196612
  330.4 19.4 %copy-start.8 = (f32[128,4,256]{2,0,1:T(8,128)S(1)}, f32[128,4,256]{2,0,1:T(8,128)}, u32[]{:S(2)}) copy-start(f32[128,4,256]{2,0,1:T(8,128)} %copy-done.7) | copy-start | bytes 1572868
  330.4 19.4 %copy-start.43 = (f32[128,4]{0,1:T(4,128)S(1)}, f32[128,4]{0,1:T(4,128)}, u32[]{:S(2)}) copy-start(f32[128,4]{0,1:T(4,128)} %copy-done.42) | copy-start | bytes 6148
  346.5 3.3 copy-start.51
  347.7 3.8 copy-start.52
  364.0 19.7 %copy-start.6 = (bf16[8,128,1152]{2,1,0:T(8,128)(2,1)S(1)}, bf16[8,128,1152]{2,1,0:T(8,128)(2,1)}, u32[]{:S(2)}) copy-start(bf16[8,128,1152]{2,1,0:T(8,128)(2,1)} %get-tuple-element.48) | copy-start | bytes 7077892
  364.1 19.7 %copy-start.63 = (f32[8,128]{1,0:T(8,128)S(1)}, f32[8,128]{1,0:T(8,128)}, u32[]{:S(2)}) copy-start(f32[8,128]{1,0:T(8,128)} %get-tuple-element.159) | copy-start | bytes 12292
  386.4 5.6 %copy-start.46 = (f32[8,4,160]{2,1,0:T(4,128)S(1)}, f32[8,4,160]{2,1,0:T(4,128)}, u32[]{:S(2)}) copy-start(f32[8,4,160]{2,1,0:T(4,128)} %get-tuple-element.63) | copy-start | bytes 61444
  459.6 5.9 %copy-start.11 = (f32[128,1152]{1,0:T(8,128)S(1)}, f32[128,1152]{1,0:T(8,128)}, u32[]{:S(2)}) copy-start(f32[128,1152]{1,0:T(8,128)} %copy-done.10) | copy-start | bytes 1769476
  459.6 5.9 %copy-start.69 = (f32[128]{0:T(128)S(1)}, f32[128]{0:T(128)}, u32[]{:S(2)}) copy-start(f32[128]{0:T(128)} %get-tuple-element.165) | copy-start | bytes 1540
  469.1 5.3 %copy-start.1 = (bf16[288,1024]{1,0:T(8,128)(2,1)S(1)}, bf16[288,1024]{1,0:T(8,128)(2,1)}, u32[]{:S(2)}) copy-start(bf16[288,1024]{1,0:T(8,128)(2,1)} %param.17) | copy-start | bytes 1769476
  (36 other events, 75.7 us)
Sparse Core Ops, SparseCore 0:
  38.9 45.2 all-gather.4
  85.8 43.9 all-gather.6
  131.3 43.9 all-gather.8
  177.6 43.8 all-gather.10
  271.8 40.3 reduce-scatter.9
  314.3 42.2 reduce-scatter.11
  359.0 47.1 reduce-scatter.13
